TPU v7x, 32 devices: a whole 2x2x4 slice. The times are simulated.
32 devices in a mesh: row: 8 (over z, y), col: 4 (over x, core).
Axes of the slice: x: 2, y: 2, z: 4, core: 2. Of those that a mesh axis runs over, the one named last changes fastest.
Arguments:
- pair: bfloat16 [768, 768, 128], P('row', 'col'), may hold values from -6 to 6
- chain_lengths: int32 [8], replicated, may hold values from 1 to 96, 576 in all
- gains: float32 [2, 2, 128], replicated, may hold values from 0.1 to 1.9
- biases: float32 [2, 2, 128], replicated, may hold values from -3 to 3
- w_in: bfloat16 [2, 128, 640], replicated, may hold values from -0.5 to 0.5
- w_out: bfloat16 [2, 128, 128], replicated, may hold values from -0.5 to 0.5
Outputs:
- pair_out: bfloat16 [768, 768, 128], P('row', 'col')
Inputs may be any that keep to these rules, and one draw needn't show every extreme that they name: Chain k occupies positions k * 96 to (k + 1) * 96 - 1 and its live residues are the first chain_lengths[k] of them; the lengths sum to 576 and one of them equals 96.
All inputs are finite; a program needn't handle non-finite values.
Results may differ from a plain program's by a relative error of at most 0.0054.
Values may be sent and summed in bfloat16 or wider, within the bound.
A program may use at most 128 MiB of HBM per device.

v0:
```python
import jax
import jax.numpy as jnp
from jax import lax
from jax.sharding import PartitionSpec as P

N = 768
NCHAIN = 8


def layer_norm(values, gain_vec, bias_vec, axis_pos):
    wide = values.astype(jnp.float32)
    average = jnp.mean(wide, axis=axis_pos, keepdims=True)
    centred = wide - average
    variance = jnp.mean(centred * centred, axis=axis_pos, keepdims=True)
    return centred * jax.lax.rsqrt(variance + 1e-05) * gain_vec + bias_vec


def live_values(global_index, chain_lengths):
    slot_size = N // NCHAIN
    chain_index = global_index // slot_size
    offset = global_index % slot_size
    matches = chain_index[:, None] == jnp.arange(NCHAIN, dtype=jnp.int32)[None, :]
    live_length = jnp.sum(jnp.where(matches, chain_lengths[None, :], 0), axis=1)
    return (offset < live_length).astype(jnp.float32)


def body(pair, chain_lengths, gains, biases, w_in, w_out):
    tile_rows, tile_cols, channels = pair.shape
    n_row = lax.axis_size("row")
    n_col = lax.axis_size("col")
    owned_count = channels // (n_row * n_col)
    row_index = lax.axis_index("row") * tile_rows + jnp.arange(tile_rows, dtype=jnp.int32)
    col_index = lax.axis_index("col") * tile_cols + jnp.arange(tile_cols, dtype=jnp.int32)
    pmask = (
        live_values(row_index, chain_lengths)[:, None]
        * live_values(col_index, chain_lengths)[None, :]
    )

    def return_products(products):
        split = products.reshape(owned_count, n_row, tile_rows, n_col, tile_cols)
        ordered = split.transpose(1, 3, 0, 2, 4).reshape(channels, tile_rows, tile_cols)
        return lax.all_to_all(ordered, ("row", "col"), split_axis=0, concat_axis=0, tiled=True)

    state = pair
    for update_index in range(2):
        weights_in = w_in[update_index]
        normed = layer_norm(state, gains[update_index, 0], biases[update_index, 0], 2).astype(
            jnp.bfloat16
        )

        def project_first(column_block):
            block = weights_in[:, column_block * channels : (column_block + 1) * channels]
            return jnp.einsum("ijc,cd->dij", normed, block, preferred_element_type=jnp.float32)

        left_edges = (pmask[None] * jax.nn.sigmoid(project_first(1)) * project_first(0)).astype(
            jnp.bfloat16
        )
        right_edges = (pmask[None] * jax.nn.sigmoid(project_first(3)) * project_first(2)).astype(
            jnp.bfloat16
        )

        def squared(block):
            split = block.reshape(owned_count, n_row, n_col, tile_rows, tile_cols)
            return split.transpose(0, 1, 3, 2, 4).reshape(
                owned_count, n_row * tile_rows, n_col * tile_cols
            )

        left_full = squared(
            lax.all_to_all(
                left_edges[:, None], ("row", "col"), split_axis=0, concat_axis=1, tiled=True
            )
        )
        right_full = squared(
            lax.all_to_all(
                right_edges[:, None], ("row", "col"), split_axis=0, concat_axis=1, tiled=True
            )
        )
        if update_index == 1:
            products = jnp.einsum(
                "cki,ckj->cij", left_full, right_full, preferred_element_type=jnp.float32
            )
        else:
            products = jnp.einsum(
                "cik,cjk->cij", left_full, right_full, preferred_element_type=jnp.float32
            )
        returned = return_products(products.astype(jnp.bfloat16))
        gain_out = gains[update_index, 1]
        bias_out = biases[update_index, 1]
        weights_out = w_out[update_index]
        normed_out = layer_norm(
            returned, gain_out[:, None, None], bias_out[:, None, None], 0
        ).astype(jnp.bfloat16)
        mixed = jnp.einsum(
            "cij,cd->ijd", normed_out, weights_out, preferred_element_type=jnp.float32
        )
        gate_vals = jax.nn.sigmoid(
            jnp.dot(
                normed.reshape(tile_rows * tile_cols, channels),
                weights_in[:, 4 * channels : 5 * channels],
                preferred_element_type=jnp.float32,
            ).reshape(tile_rows, tile_cols, channels)
        )
        state = (state.astype(jnp.float32) + gate_vals * mixed).astype(jnp.bfloat16)
    return state


def solution(mesh):
    placed = (P("row", "col", None), P(), P(), P(), P(), P())
    return jax.shard_map(
        body, mesh=mesh, in_specs=placed, out_specs=P("row", "col", None), check_vma=False
    )
```

profile of v0, /device:TPU:0, one launch (start us, length us, event | category | flops | bytes accessed | tf_op | source)
XLA Modules:
  0.0 1077.4 jit_solution(6276886250973530438)
XLA Ops:
  0.0 0.8 select_reduce_fusion.1
  0.9 0.9 select_reduce_fusion
  1.8 4.4 convert_reduce_fusion.3
  6.1 7.7 fusion.20
  13.8 0.0 copy-done.2
  13.9 0.6 slice_bitcast_fusion.22
  14.5 0.1 add_rsqrt_fusion.3
  14.6 5.1 fusion.36
  19.6 10.7 fusion.31
  30.3 9.0 copy.39
  39.4 7.5 all-to-all-start.1
  46.9 0.0 slice-start.1
  46.9 10.5 fusion.37
  57.5 10.7 fusion.30
  68.2 9.1 copy.37
  77.2 109.4 %all-to-all-done.1 = bf16[128,1,96,192]{3,2,1,0:T(8,128)(2,1)} async-done(((bf16[128,1,96,192]{3,2,1,0:T(8,128)(2,1)}), bf16[128,1,96,192]{3,2,1,0:T(8,128)(2,1)}, u32[]{:S(2)}, u32[]{:S(2)}) %all-to-all-start.1) | async-done | bytes 4718624 | tf_op jit(solution)/shard_map/all_to_all | solution.py:74
  186.6 3.8 all-to-all-start
  190.4 11.3 %copy.57 = bf16[4,8,4,96,192]{4,2,3,1,0:T(4,128)(2,1)} copy(bf16[4,8,4,96,192]{4,3,0,2,1:T(8,128)(2,1)} %bitcast.18) | data formatting | bytes 9437184 | tf_op jit(solution)/shard_map/reshape | solution.py:63
  201.7 11.8 %reshape.179 = bf16[4,768,768]{2,1,0:T(8,128)(2,1)} reshape(bf16[4,8,96,4,192]{4,3,2,1,0:T(4,128)(2,1)} %bitcast.130) | data formatting | bytes 9437184 | tf_op jit(solution)/shard_map/reshape | solution.py:64
  213.4 116.7 %all-to-all-done = bf16[128,1,96,192]{3,2,1,0:T(8,128)(2,1)} async-done(((bf16[128,1,96,192]{3,2,1,0:T(8,128)(2,1)}), bf16[128,1,96,192]{3,2,1,0:T(8,128)(2,1)}, u32[]{:S(2)}, u32[]{:S(2)}) %all-to-all-start) | async-done | bytes 4718624 | tf_op jit(solution)/shard_map/all_to_all | solution.py:69
  330.2 11.3 %copy.58 = bf16[4,8,4,96,192]{4,2,3,1,0:T(4,128)(2,1)} copy(bf16[4,8,4,96,192]{4,3,0,2,1:T(8,128)(2,1)} %bitcast.10) | data formatting | bytes 9437184 | tf_op jit(solution)/shard_map/reshape | solution.py:63
  341.4 11.6 %reshape.177 = bf16[4,768,768]{2,1,0:T(8,128)(2,1)} reshape(bf16[4,8,96,4,192]{4,3,2,1,0:T(4,128)(2,1)} %bitcast.131) | data formatting | bytes 9437184 | tf_op jit(solution)/shard_map/reshape | solution.py:64
  353.0 9.9 convolution_convert_fusion.1
  362.9 12.9 %reshape.180 = bf16[4,8,96,4,192]{4,3,2,1,0:T(4,128)(2,1)} reshape(bf16[4,768,768]{2,1,0:T(8,128)(2,1)} %convolution_convert_fusion.1) | data formatting | bytes 9437184 | tf_op jit(solution)/shard_map/reshape | solution.py:40
  375.8 4.0 copy.41
  379.8 141.3 %all_to_all.70 = bf16[128,96,192]{2,1,0:T(8,128)(2,1)S(1)} all-to-all(bf16[128,96,192]{2,1,0:T(8,128)(2,1)S(1)} %bitcast.128), channel_id=1, replica_groups=mesh['row'=8,'col'=4] {'row','col'}, dimensions={0} | all-to-all | bytes 9437184 | tf_op jit(solution)/shard_map/all_to_all | solution.py:42
  521.1 1.1 convert_reduce_fusion.1
  522.2 0.0 copy-start.3
  522.2 1.9 fusion.8
  524.1 0.0 slice-start.2
  524.2 4.0 fusion.11
  528.2 0.0 slice-start.3
  528.2 6.0 fusion.28
  534.2 10.1 convert_reduce_fusion.2
  544.4 0.0 copy-start.1
  544.4 6.6 fusion.16
  551.0 5.1 fusion.35
  556.1 10.7 fusion.32
  566.8 9.1 copy.43
  575.9 3.8 all-to-all-start.3
  579.8 0.0 slice-start.5
  579.8 10.5 fusion.34
  590.4 10.8 fusion.33
  601.1 9.0 copy.45
  610.2 109.4 %all-to-all-done.3 = bf16[128,1,96,192]{3,2,1,0:T(8,128)(2,1)} async-done(((bf16[128,1,96,192]{3,2,1,0:T(8,128)(2,1)}), bf16[128,1,96,192]{3,2,1,0:T(8,128)(2,1)}, u32[]{:S(2)}, u32[]{:S(2)}) %all-to-all-start.3) | async-done | bytes 4718624 | tf_op jit(solution)/shard_map/all_to_all | solution.py:69
  719.5 3.8 all-to-all-start.4
  723.4 9.2 copy.44
  732.5 10.8 %reshape.183 = bf16[4,768,768]{1,2,0:T(8,128)(2,1)} reshape(bf16[4,8,96,4,192]{2,1,4,3,0:T(8,128)(2,1)} %bitcast.132) | data formatting | bytes 9437184 | tf_op jit(solution)/shard_map/reshape | solution.py:64
  743.4 119.7 %all-to-all-done.4 = bf16[128,1,96,192]{3,2,1,0:T(8,128)(2,1)} async-done(((bf16[128,1,96,192]{3,2,1,0:T(8,128)(2,1)}), bf16[128,1,96,192]{3,2,1,0:T(8,128)(2,1)}, u32[]{:S(2)}, u32[]{:S(2)}) %all-to-all-start.4) | async-done | bytes 4718624 | tf_op jit(solution)/shard_map/all_to_all | solution.py:74
  863.1 11.3 %copy.56 = bf16[4,8,4,96,192]{4,2,3,1,0:T(4,128)(2,1)} copy(bf16[4,8,4,96,192]{4,3,0,2,1:T(8,128)(2,1)} %bitcast.44) | data formatting | bytes 9437184 | tf_op jit(solution)/shard_map/reshape | solution.py:63
  874.4 11.6 %reshape.185 = bf16[4,768,768]{2,1,0:T(8,128)(2,1)} reshape(bf16[4,8,96,4,192]{4,3,2,1,0:T(4,128)(2,1)} %bitcast.133) | data formatting | bytes 9437184 | tf_op jit(solution)/shard_map/reshape | solution.py:64
  886.0 9.7 convolution_convert_fusion
  895.7 12.9 %reshape.186 = bf16[4,8,96,4,192]{4,3,2,1,0:T(4,128)(2,1)} reshape(bf16[4,768,768]{2,1,0:T(8,128)(2,1)} %convolution_convert_fusion) | data formatting | bytes 9437184 | tf_op jit(solution)/shard_map/reshape | solution.py:40
  908.6 4.0 copy.47
  912.6 141.5 %all_to_all.71 = bf16[128,96,192]{2,1,0:T(8,128)(2,1)S(1)} all-to-all(bf16[128,96,192]{2,1,0:T(8,128)(2,1)S(1)} %bitcast.129), channel_id=1, replica_groups=mesh['row'=8,'col'=4] {'row','col'}, dimensions={0} | all-to-all | bytes 9437184 | tf_op jit(solution)/shard_map/all_to_all | solution.py:42
  1054.2 1.1 convert_reduce_fusion
  1055.3 1.9 fusion.4
  1057.2 0.0 slice-start.6
  1057.2 4.0 fusion.7
  1061.2 0.0 slice-start.7
  1061.3 6.0 fusion.26
  1067.3 0.0 slice-done.6
  1067.3 0.0 slice-done.7
  1067.3 9.6 fusion.25
  (37 shorter events, 0.2 us)
Async XLA Ops:
  0.0 13.8 %copy-start.2 = (bf16[2,128,640]{2,1,0:T(8,128)(2,1)S(1)}, bf16[2,128,640]{2,1,0:T(8,128)(2,1)}, u32[]{:S(2)}) copy-start(bf16[2,128,640]{2,1,0:T(8,128)(2,1)} %param.10) | copy-start | bytes 983044
  0.0 13.9 %copy-start.6 = (f32[2,2,128]{2,1,0:T(2,128)S(1)}, f32[2,2,128]{2,1,0:T(2,128)}, u32[]{:S(2)}) copy-start(f32[2,2,128]{2,1,0:T(2,128)} %param.9) | copy-start | bytes 6148
  0.0 13.9 %copy-start.7 = (f32[2,2,128]{2,1,0:T(2,128)S(1)}, f32[2,2,128]{2,1,0:T(2,128)}, u32[]{:S(2)}) copy-start(f32[2,2,128]{2,1,0:T(2,128)} %param.8) | copy-start | bytes 6148
  0.8 13.7 %copy-start = (bf16[96,192,128]{2,1,0:T(8,128)(2,1)S(1)}, bf16[96,192,128]{2,1,0:T(8,128)(2,1)}, u32[]{:S(2)}) copy-start(bf16[96,192,128]{2,1,0:T(8,128)(2,1)} %param.6) | copy-start | bytes 14155780
  39.4 18.0 %slice-start = ((s8[4718592]{0:T(1024)(128)(4,1)}), s8[524288]{0:T(1024)(128)(4,1)S(1)}, s32[]{:S(2)}) async-start(s8[4718592]{0:T(1024)(128)(4,1)} %bitcast.120), calls=%async_computation.6 | async-start | bytes 1048576
  39.4 147.2 %all-to-all-start.1 = ((bf16[128,1,96,192]{3,2,1,0:T(8,128)(2,1)}), bf16[128,1,96,192]{3,2,1,0:T(8,128)(2,1)}, u32[]{:S(2)}, u32[]{:S(2)}) async-start(bf16[128,1,96,192]{3,2,1,0:T(8,128)(2,1)} %copy.39), calls=%async_computation.1 | async-start | bytes 12582912 | tf_op jit(solution)/shard_map/all_to_all | solution.py:74
  46.9 10.6 slice-start.1
  186.6 143.5 %all-to-all-start = ((bf16[128,1,96,192]{3,2,1,0:T(8,128)(2,1)}), bf16[128,1,96,192]{3,2,1,0:T(8,128)(2,1)}, u32[]{:S(2)}, u32[]{:S(2)}) async-start(bf16[128,1,96,192]{3,2,1,0:T(8,128)(2,1)} %copy.37), calls=%async_computation | async-start | bytes 12582912 | tf_op jit(solution)/shard_map/all_to_all | solution.py:69
  522.2 5.9 copy-start.3
  524.1 10.1 slice-start.2
  528.2 6.0 slice-start.3
  544.4 11.7 %copy-start.1 = (bf16[96,192,128]{2,1,0:T(8,128)(2,1)}, bf16[96,192,128]{2,1,0:T(8,128)(2,1)S(1)}, u32[]{:S(2)}) copy-start(bf16[96,192,128]{2,1,0:T(8,128)(2,1)S(1)} %get-tuple-element.16) | copy-start | bytes 14155780
  575.9 14.4 %slice-start.4 = ((s8[4718592]{0:T(1024)(128)(4,1)}), s8[524288]{0:T(1024)(128)(4,1)S(1)}, s32[]{:S(2)}) async-start(s8[4718592]{0:T(1024)(128)(4,1)} %bitcast.124), calls=%async_computation.10 | async-start | bytes 1048576
  575.9 143.6 %all-to-all-start.3 = ((bf16[128,1,96,192]{3,2,1,0:T(8,128)(2,1)}), bf16[128,1,96,192]{3,2,1,0:T(8,128)(2,1)}, u32[]{:S(2)}, u32[]{:S(2)}) async-start(bf16[128,1,96,192]{3,2,1,0:T(8,128)(2,1)} %copy.43), calls=%async_computation.3 | async-start | bytes 12582912 | tf_op jit(solution)/shard_map/all_to_all | solution.py:69
  579.8 10.6 slice-start.5
  719.5 143.6 %all-to-all-start.4 = ((bf16[128,1,96,192]{3,2,1,0:T(8,128)(2,1)}), bf16[128,1,96,192]{3,2,1,0:T(8,128)(2,1)}, u32[]{:S(2)}, u32[]{:S(2)}) async-start(bf16[128,1,96,192]{3,2,1,0:T(8,128)(2,1)} %copy.45), calls=%async_computation.4 | async-start | bytes 12582912 | tf_op jit(solution)/shard_map/all_to_all | solution.py:74
  1054.2 3.0 copy-start.4
  1054.2 3.1 copy-start.5
  1057.2 10.0 slice-start.6
  1061.2 6.0 slice-start.7
where the time goes:
time: 1090 us; the launch traced here: 1080 us
  waiting for transfers between devices  455 us (42%)
  blocking collectives  283 us (26%)
  local copies, waits for them, and re-layouts  160 us (15%)
  matrix products  126 us (12%)
  other arithmetic  34.5 us (3%)
  starting transfers between devices  18.9 us (2%)
    all_to_all x2, blocking collectives, return_products(): lax.all_to_all(ordered, ('row', 'col'), split_axis=0, concat_axis=0, tile...  283 us
    all_to_all x2, waiting for transfers between devices, body(): lax.all_to_all(right_edges[:, None], ('row', 'col'), split_axis=0, concat...  229 us
    all_to_all x2, waiting for transfers between devices, body(): lax.all_to_all(left_edges[:, None], ('row', 'col'), split_axis=0, concat_...  226 us
    dot_general x8, matrix products, project_first(): jnp.einsum('ijc,cd->dij', normed, block, preferred_element_type=jnp.float32)  74.2 us
    reshape x4, local copies, waits for them, and re-layouts, squared(): split.transpose(0, 1, 3, 2, 4)  45.8 us
    reshape x4, local copies, waits for them, and re-layouts, squared(): split = block.reshape(owned_count, n_row, n_col, tile_rows, tile_cols)  43 us
    reshape x4, local copies, waits for them, and re-layouts, return_products(): split = products.reshape(owned_count, n_row, tile_rows, n_col, tile_cols)  33.8 us
  transfers between devices with their start and end apart: 4, of which 4 were waited for; matrix products, arithmetic and copies ran while one was open for 10% of the time, Pallas kernels for 0%

commit v1 on v0

--- a/solution.py
+++ b/solution.py
@@ -1,10 +1,14 @@
+import functools
+
 import jax
 import jax.numpy as jnp
 from jax import lax
+from jax.experimental import pallas as pl
+from jax.experimental.pallas import tpu as pltpu
 from jax.sharding import PartitionSpec as P
 
-N = 768
-NCHAIN = 8
+LANES = 128
+HALF = LANES // 2
 
 
 def layer_norm(values, gain_vec, bias_vec, axis_pos):
@@ -15,25 +19,201 @@
     return centred * jax.lax.rsqrt(variance + 1e-05) * gain_vec + bias_vec
 
 
-def live_values(global_index, chain_lengths):
-    slot_size = N // NCHAIN
+def live_values(global_index, chain_lengths, total):
+    n_chain = chain_lengths.shape[0]
+    slot_size = total // n_chain
     chain_index = global_index // slot_size
     offset = global_index % slot_size
-    matches = chain_index[:, None] == jnp.arange(NCHAIN, dtype=jnp.int32)[None, :]
+    matches = chain_index[:, None] == jnp.arange(n_chain, dtype=jnp.int32)[None, :]
     live_length = jnp.sum(jnp.where(matches, chain_lengths[None, :], 0), axis=1)
     return (offset < live_length).astype(jnp.float32)
+
+
+def segments(start, length, tile_cols, n_col):
+    runs, at = [], start
+    while at < start + length:
+        block, inside = divmod(at, tile_cols)
+        if inside < LANES:
+            stop, packed = block * tile_cols + LANES, block * LANES + inside
+        else:
+            stop, packed = (block + 1) * tile_cols, n_col * LANES + block * HALF + inside - LANES
+        stop = min(stop, start + length)
+        runs.append((at - start, packed, stop - at))
+        at = stop
+    return runs
+
+
+def join(first, second, upper):
+    lanes = slice(HALF, LANES) if upper else slice(0, HALF)
+    return jnp.concatenate([first[:, lanes], second[:, lanes]], axis=1)
+
+
+def triangle_kernel(geometry, incoming, left_ref, right_ref, out_ref, left, right, tri):
+    n_row, n_col, rows, cols = geometry
+    half = rows // 2
+
+    def unpack(source, target, packed_rows):
+        for r in range(n_row):
+            if packed_rows:
+                runs = segments(r * rows, rows, cols, n_col)
+            else:
+                runs = [(0, r * rows, rows)]
+
+            def put(offset, block, lane_at):
+                size = block.shape[0]
+                for begin, packed, length in runs:
+                    lo, hi = max(begin, offset), min(begin + length, offset + size)
+                    if lo < hi:
+                        target[packed + lo - begin:packed + hi - begin, lane_at:lane_at + LANES] = (
+                            block[lo - offset:hi - offset]
+                        )
+
+            for s in range(n_col):
+                put(0, source[r, s, 0, :rows, :], s * LANES)
+            for p in range(n_col // 2):
+                first = source[r, 2 * p, 0, rows:, :]
+                second = source[r, 2 * p + 1, 0, rows:, :]
+                lane_at = (n_col + p) * LANES
+                put(0, join(first, second, False), lane_at)
+                put(half, join(first, second, True), lane_at)
+
+    unpack(left_ref, left, False)
+    unpack(right_ref, right, not incoming)
+    contract = ((0,), (0,)) if incoming else ((1,), (1,))
+    tri[...] = lax.dot_general(
+        left[...], right[...], (contract, ((), ())), preferred_element_type=jnp.float32
+    ).astype(tri.dtype)
+
+    for r in range(n_row):
+        if incoming:
+            runs = segments(r * rows, rows, cols, n_col)
+        else:
+            runs = [(0, r * rows, rows)]
+
+        def get(offset, size, lane_at):
+            parts = []
+            for begin, packed, length in runs:
+                lo, hi = max(begin, offset), min(begin + length, offset + size)
+                if lo < hi:
+                    parts.append(
+                        tri[packed + lo - begin:packed + hi - begin, lane_at:lane_at + LANES]
+                    )
+            return parts[0] if len(parts) == 1 else jnp.concatenate(parts, axis=0)
+
+        for s in range(n_col):
+            out_ref[r, s, 0, :rows, :] = get(0, rows, s * LANES)
+        for p in range(n_col // 2):
+            lane_at = (n_col + p) * LANES
+            above, below = get(0, half, lane_at), get(half, half, lane_at)
+            out_ref[r, 2 * p, 0, rows:, :] = join(above, below, False)
+            out_ref[r, 2 * p + 1, 0, rows:, :] = join(above, below, True)
+
+
+def triangle(left, right, geometry, incoming):
+    n_row, n_col, rows, cols = geometry
+    owned, packed, lanes = left.shape[0] // (n_row * n_col), left.shape[1], left.shape[2]
+    total = n_row * rows
+    shape = (n_row, n_col, owned, packed, lanes)
+    spec = pl.BlockSpec((n_row, n_col, 1, packed, lanes), lambda c: (0, 0, c, 0, 0))
+    out = pl.pallas_call(
+        functools.partial(triangle_kernel, geometry, incoming),
+        grid=(owned,),
+        in_specs=[spec, spec],
+        out_specs=spec,
+        out_shape=jax.ShapeDtypeStruct(shape, jnp.bfloat16),
+        scratch_shapes=[pltpu.VMEM((total, total), jnp.bfloat16)] * 3,
+        cost_estimate=pl.CostEstimate(
+            flops=2 * owned * total**3, bytes_accessed=6 * left.size, transcendentals=0
+        ),
+        compiler_params=pltpu.CompilerParams(vmem_limit_bytes=48 * 2**20),
+        name="triangle_in" if incoming else "triangle_out",
+    )(left.reshape(shape), right.reshape(shape))
+    return out.reshape(left.shape)
+
+
+def pack_tile(tile):
+    rows, _, channels = tile.shape
+    tail = tile[:, LANES:].reshape(2, rows // 2, HALF, channels).transpose(1, 0, 2, 3)
+    return jnp.concatenate([tile[:, :LANES], tail.reshape(rows // 2, LANES, channels)], axis=0)
+
+
+def unpack_tile(packed, rows):
+    channels = packed.shape[2]
+    tail = packed[rows:].reshape(rows // 2, 2, HALF, channels).transpose(1, 0, 2, 3)
+    return jnp.concatenate([packed[:rows], tail.reshape(rows, HALF, channels)], axis=1)
+
+
+def packed_body(pair, chain_lengths, gains, biases, w_in, w_out):
+    tile_rows, tile_cols, channels = pair.shape
+    n_row = lax.axis_size("row")
+    n_col = lax.axis_size("col")
+    geometry = (n_row, n_col, tile_rows, tile_cols)
+    total = n_row * tile_rows
+    row_index = lax.axis_index("row") * tile_rows + jnp.arange(tile_rows, dtype=jnp.int32)
+    col_index = lax.axis_index("col") * tile_cols + jnp.arange(tile_cols, dtype=jnp.int32)
+    pmask = (
+        live_values(row_index, chain_lengths, total)[:, None]
+        * live_values(col_index, chain_lengths, total)[None, :]
+    )
+    pmask = pack_tile(pmask[:, :, None])[:, :, 0]
+
+    def exchange(block):
+        return lax.all_to_all(block, ("row", "col"), split_axis=0, concat_axis=0, tiled=True)
+
+    state = pack_tile(pair)
+    for update_index in range(2):
+        weights_in = w_in[update_index]
+        normed = layer_norm(state, gains[update_index, 0], biases[update_index, 0], 2).astype(
+            jnp.bfloat16
+        )
+
+        def project_first(column_block):
+            block = weights_in[:, column_block * channels : (column_block + 1) * channels]
+            return jnp.einsum("ijc,cd->dij", normed, block, preferred_element_type=jnp.float32)
+
+        left_edges = (pmask[None] * jax.nn.sigmoid(project_first(1)) * project_first(0)).astype(
+            jnp.bfloat16
+        )
+        right_edges = (pmask[None] * jax.nn.sigmoid(project_first(3)) * project_first(2)).astype(
+            jnp.bfloat16
+        )
+        products = triangle(
+            exchange(left_edges), exchange(right_edges), geometry, update_index == 1
+        )
+        returned = exchange(products)
+        gain_out = gains[update_index, 1]
+        bias_out = biases[update_index, 1]
+        normed_out = layer_norm(
+            returned, gain_out[:, None, None], bias_out[:, None, None], 0
+        ).astype(jnp.bfloat16)
+        mixed = jnp.einsum(
+            "cij,cd->ijd", normed_out, w_out[update_index], preferred_element_type=jnp.float32
+        )
+        gate_vals = jax.nn.sigmoid(
+            jnp.einsum(
+                "ijc,cd->ijd",
+                normed,
+                weights_in[:, 4 * channels : 5 * channels],
+                preferred_element_type=jnp.float32,
+            )
+        )
+        state = (state.astype(jnp.float32) + gate_vals * mixed).astype(jnp.bfloat16)
+    return unpack_tile(state, tile_rows)
 
 
 def body(pair, chain_lengths, gains, biases, w_in, w_out):
     tile_rows, tile_cols, channels = pair.shape
     n_row = lax.axis_size("row")
     n_col = lax.axis_size("col")
+    if tile_cols == LANES + HALF and tile_rows % 32 == 0 and tile_cols % tile_rows == 0 and n_col % 2 == 0:
+        return packed_body(pair, chain_lengths, gains, biases, w_in, w_out)
     owned_count = channels // (n_row * n_col)
+    total = n_row * tile_rows
     row_index = lax.axis_index("row") * tile_rows + jnp.arange(tile_rows, dtype=jnp.int32)
     col_index = lax.axis_index("col") * tile_cols + jnp.arange(tile_cols, dtype=jnp.int32)
     pmask = (
-        live_values(row_index, chain_lengths)[:, None]
-        * live_values(col_index, chain_lengths)[None, :]
+        live_values(row_index, chain_lengths, total)[:, None]
+        * live_values(col_index, chain_lengths, total)[None, :]
     )
 
     def return_products(products):
@@ -75,23 +255,18 @@
                 right_edges[:, None], ("row", "col"), split_axis=0, concat_axis=1, tiled=True
             )
         )
-        if update_index == 1:
-            products = jnp.einsum(
-                "cki,ckj->cij", left_full, right_full, preferred_element_type=jnp.float32
-            )
-        else:
-            products = jnp.einsum(
-                "cik,cjk->cij", left_full, right_full, preferred_element_type=jnp.float32
-            )
+        equation = "cki,ckj->cij" if update_index == 1 else "cik,cjk->cij"
+        products = jnp.einsum(
+            equation, left_full, right_full, preferred_element_type=jnp.float32
+        )
         returned = return_products(products.astype(jnp.bfloat16))
         gain_out = gains[update_index, 1]
         bias_out = biases[update_index, 1]
-        weights_out = w_out[update_index]
         normed_out = layer_norm(
             returned, gain_out[:, None, None], bias_out[:, None, None], 0
         ).astype(jnp.bfloat16)
         mixed = jnp.einsum(
-            "cij,cd->ijd", normed_out, weights_out, preferred_element_type=jnp.float32
+            "cij,cd->ijd", normed_out, w_out[update_index], preferred_element_type=jnp.float32
         )
         gate_vals = jax.nn.sigmoid(
             jnp.dot(

time: 1090 us -> 782 us (0.72); the launches traced: 1080 us -> 781 us
  waiting for transfers between devices: 455 us -> 153 us
  blocking collectives: 283 us -> 435 us
  local copies, waits for them, and re-layouts: 160 us -> 38.7 us
  matrix products: 126 us -> 99.4 us
  Pallas kernels: 0 us -> 16.7 us
    all_to_all x4 -> x2, waiting for transfers between devices: 455 us -> 153 us  [exchange(): lax.all_to_all(block, ('row', 'col'), split_axis=0, concat_axis=0, tiled=...]
    all_to_all x2 -> x4, blocking collectives: 283 us -> 435 us  [exchange(): lax.all_to_all(block, ('row', 'col'), split_axis=0, concat_axis=0, tiled=...]
    reshape x12 -> x3, local copies, waits for them, and re-layouts: 123 us -> 1.73 us  [the longest x2 1.64 us: pack_tile(): tile[:, LANES:].reshape(2, rows // 2, HALF, channels).transpose(1, 0, 2, 3)]
    broadcast_in_dim x4 -> x0, local copies, waits for them, and re-layouts: 36.2 us -> none  [the longest x2 18.2 us: body(): left_edges[:, None]]
    dot_general x6 -> x4, matrix products: 51.3 us -> 22.4 us  [the longest x2 19.6 us: packed_body(): jnp.einsum('ijc,cd->ijd', normed, weights_in[:, 4 * channels:5 * channels...]
    convert_element_type x0 -> x4, local copies, waits for them, and re-layouts: none -> 28 us  [the longest x2 14 us: packed_body(): (pmask[None] * jax.nn.sigmoid(project_first(3)) * project_first(2)).astyp...]
    pallas_call x0 -> x2, Pallas kernels: none -> 16.7 us  [triangle(): pl.pallas_call(functools.partial(triangle_kernel, geometry, incoming), gr...]
  transfers between devices with their start and end apart: 4 -> 2, of which waited for: 4 -> 2; matrix products, arithmetic and copies ran while one was open for 10% -> 7% of each run, Pallas kernels for 0% -> 0%
where the time goes in v1:
time: 782 us; the launch traced here: 781 us
  blocking collectives  435 us (56%)
  waiting for transfers between devices  153 us (20%)
  matrix products  99.4 us (13%)
  local copies, waits for them, and re-layouts  38.7 us (5%)
  other arithmetic  25.4 us (3%)
  Pallas kernels  16.7 us (2%)
  starting transfers between devices  11.4 us (1%)
    all_to_all x4, blocking collectives, exchange(): lax.all_to_all(block, ('row', 'col'), split_axis=0, concat_axis=0, tiled=...  435 us
    all_to_all x2, waiting for transfers between devices, exchange(): lax.all_to_all(block, ('row', 'col'), split_axis=0, concat_axis=0, tiled=...  153 us
    dot_general x8, matrix products, project_first(): jnp.einsum('ijc,cd->dij', normed, block, preferred_element_type=jnp.float32)  77 us
    dot_general x2, matrix products, packed_body(): jnp.einsum('ijc,cd->ijd', normed, weights_in[:, 4 * channels:5 * channels...  19.6 us
    pallas_call x2, Pallas kernels, triangle(): pl.pallas_call(functools.partial(triangle_kernel, geometry, incoming), gr...  16.7 us
  transfers between devices with their start and end apart: 2, of which 2 were waited for; matrix products, arithmetic and copies ran while one was open for 7% of the time, Pallas kernels for 0%

profile of v1, /device:TPU:0, one launch (start us, length us, event | category | flops | bytes accessed | tf_op | source)
XLA Modules:
  0.0 781.0 jit_solution(8117064709006675616)
XLA Ops:
  0.0 0.8 select_reduce_fusion.1
  0.8 0.7 select_reduce_fusion
  1.6 0.1 broadcast_multiply_fusion
  1.7 0.6 slice.113
  2.3 2.7 slice.85
  5.0 2.1 slice.84
  7.2 0.1 reshape.184
  7.2 0.0 copy-done.4
  7.3 0.7 slice_bitcast_fusion
  7.9 1.6 copy.25
  9.6 0.0 copy-start.1
  9.6 1.3 convert_reduce_fusion.1
  10.9 6.0 fusion.12
  16.9 0.0 copy-start.11
  16.9 1.4 slice_bitcast_fusion.22
  18.4 0.0 copy-done.6
  18.4 0.0 copy-start.9
  18.4 5.1 fusion.37
  23.5 0.0 copy-done.1
  23.5 13.4 %fusion.30 = bf16[128,144,128]{0,2,1:T(8,128)(2,1)} fusion(f32[144,128,128]{2,1,0:T(8,128)S(1)} %fusion.37, f32[144,128]{1,0:T(8,128)S(1)} %maximum_bitcast_fusion, bf16[128,640]{1,0:T(8,128)(2,1)S(1)} %get-tuple-element.6, f32[128]{0:T(128)S(1)} %get-tuple-element.13, f32[128]{0:T(128)S(1)} %get-tuple-element.18, f32[144,128]{1,0:T(8,128)S(1)} %add_rsqrt_fusion.3, ...), kind=kOutput, calls=%fused_computation.46 | convolution fusion | flops 634650624 | bytes 19129344 | tf_op jit(solution)/shard_map/ijc,cd->dij/dot_general | solution.py:172
  36.9 7.0 copy.27
  43.9 7.4 all-to-all-start
  51.4 8.0 %fusion.36 = f32[144,128,128]{2,1,0:T(8,128)S(1)} fusion(bf16[128,640]{1,0:T(8,128)(2,1)S(1)} %copy-done.8, f32[128]{0:T(128)S(1)} %get-tuple-element.13, f32[128]{0:T(128)S(1)} %get-tuple-element.18, f32[144,128]{1,0:T(8,128)S(1)} %add_rsqrt_fusion.3, f32[144,128]{1,0:T(8,128)S(1)} %broadcast_multiply_fusion.4, bf16[48,128,128]{2,1,0:T(8,128)(2,1)} %bitcast.102, ...), kind=kOutput, calls=%fused_computation.72 | convolution fusion | flops 620494848 | bytes 14337024 | tf_op jit(solution)/shard_map/ijc,cd->dij/dot_general | solution.py:172
  59.4 13.3 %fusion.31 = bf16[128,144,128]{0,2,1:T(8,128)(2,1)} fusion(f32[144,128,128]{2,1,0:T(8,128)S(1)} %fusion.36, f32[144,128]{1,0:T(8,128)S(1)} %maximum_bitcast_fusion, bf16[128,640]{1,0:T(8,128)(2,1)S(1)} %copy-done.8, f32[128]{0:T(128)S(1)} %get-tuple-element.13, f32[128]{0:T(128)S(1)} %get-tuple-element.18, f32[144,128]{1,0:T(8,128)S(1)} %add_rsqrt_fusion.3, ...), kind=kOutput, calls=%fused_computation.47 | convolution fusion | flops 634650624 | bytes 19129344 | tf_op jit(solution)/shard_map/ijc,cd->dij/dot_general | solution.py:172
  72.8 7.0 copy.28
  79.8 76.7 %all-to-all-done = bf16[128,144,128]{2,1,0:T(8,128)(2,1)} async-done(((bf16[128,144,128]{2,1,0:T(8,128)(2,1)}), bf16[128,144,128]{2,1,0:T(8,128)(2,1)}, u32[]{:S(2)}, u32[]{:S(2)}) %all-to-all-start) | async-done | bytes 4718624 | tf_op jit(solution)/shard_map/all_to_all | solution.py:161
  156.4 109.6 %all_to_all.30 = bf16[128,144,128]{2,1,0:T(8,128)(2,1)} all-to-all(bf16[128,144,128]{2,1,0:T(8,128)(2,1)} %copy.28), channel_id=1, replica_groups=mesh['row'=8,'col'=4] {'row','col'}, dimensions={0} | all-to-all | bytes 9437184 | tf_op jit(solution)/shard_map/all_to_all | solution.py:161
  266.0 7.9 %triangle_out.1 = bf16[8,4,4,144,128]{4,3,2,1,0:T(8,128)(2,1)S(1)} custom-call(bf16[8,4,4,144,128]{4,3,2,1,0:T(8,128)(2,1)} %bitcast.13.left_ref, bf16[8,4,4,144,128]{4,3,2,1,0:T(8,128)(2,1)} %bitcast.96), custom_call_target="tpu_custom_call" | custom-call | flops 3623878656 | bytes 14155776 | tf_op jit(solution)/shard_map/triangle_out/pallas_call | solution.py:118
  273.9 108.3 %all_to_all.31 = bf16[128,144,128]{2,1,0:T(8,128)(2,1)S(1)} all-to-all(bf16[128,144,128]{2,1,0:T(8,128)(2,1)S(1)} %bitcast.90), channel_id=1, replica_groups=mesh['row'=8,'col'=4] {'row','col'}, dimensions={0} | all-to-all | bytes 9437184 | tf_op jit(solution)/shard_map/all_to_all | solution.py:161
  382.2 0.7 convert_reduce_fusion.3
  382.9 1.3 fusion.20
  384.2 2.2 fusion.23
  386.5 1.4 fusion.28
  388.0 10.4 %convert_reduce_fusion = (f32[144,128]{1,0:T(8,128)S(1)}, bf16[144,128,128]{2,1,0:T(8,128)(2,1)S(1)}) fusion(f32[144,128,128]{2,1,0:T(8,128)S(1)} %fusion.28, bf16[128,640]{1,0:T(8,128)(2,1)S(1)} %copy-done.8, f32[128]{0:T(128)S(1)} %copy-done.18, f32[128]{0:T(128)S(1)} %copy-done.20, f32[144,128]{1,0:T(8,128)S(1)} %copy-done.12, ...), kind=kOutput, calls=%fused_computation.2 | convolution fusion | flops 644069376 | bytes 23847936 | tf_op jit(solution)/shard_map/ijc,cd->ijd/dot_general | solution.py:193
  398.4 0.0 copy-start
  398.4 5.4 fusion.8
  403.9 5.1 fusion.35
  409.0 10.8 %fusion.32 = bf16[128,144,128]{0,2,1:T(8,128)(2,1)} fusion(f32[144,128,128]{2,1,0:T(8,128)S(1)} %fusion.35, f32[144,128]{1,0:T(8,128)S(1)} %copy-done.10, bf16[128,640]{1,0:T(8,128)(2,1)S(1)} %copy-done.5, bf16[144,128,128]{2,1,0:T(8,128)(2,1)S(1)} %get-tuple-element.16, f32[128]{0:T(128)S(1)} %get-tuple-element.14, f32[128]{0:T(128)S(1)} %get-tuple-element.17, ...), kind=kOutput, calls=%fused_computation.48 | convolution fusion | flops 632291328 | bytes 19129344 | tf_op jit(solution)/shard_map/ijc,cd->dij/dot_general | solution.py:172
  419.8 7.0 copy.30
  426.8 3.9 all-to-all-start.3
  430.7 0.0 slice-start.1
  430.7 10.5 %fusion.34 = f32[144,128,128]{2,1,0:T(8,128)S(1)} fusion(bf16[128,640]{1,0:T(8,128)(2,1)S(1)} %copy-done.5, bf16[144,128,128]{2,1,0:T(8,128)(2,1)} %copy-done, f32[128]{0:T(128)S(1)} %get-tuple-element.14, f32[128]{0:T(128)S(1)} %get-tuple-element.17, f32[144,128]{1,0:T(8,128)S(1)} %add_rsqrt_fusion.1, f32[144,128]{1,0:T(8,128)S(1)} %broadcast_multiply_fusion.2), kind=kOutput, calls=%fused_computation.65 | convolution fusion | flops 618135552 | bytes 14337024 | tf_op jit(solution)/shard_map/ijc,cd->dij/dot_general | solution.py:172
  441.3 10.8 %fusion.33 = bf16[128,144,128]{0,2,1:T(8,128)(2,1)} fusion(f32[144,128,128]{2,1,0:T(8,128)S(1)} %fusion.34, f32[144,128]{1,0:T(8,128)S(1)} %copy-done.10, bf16[128,640]{1,0:T(8,128)(2,1)S(1)} %copy-done.5, bf16[144,128,128]{2,1,0:T(8,128)(2,1)S(1)} %bitcast.93, f32[128]{0:T(128)S(1)} %get-tuple-element.14, f32[128]{0:T(128)S(1)} %get-tuple-element.17, ...), kind=kOutput, calls=%fused_computation.49 | convolution fusion | flops 632291328 | bytes 19129344 | tf_op jit(solution)/shard_map/ijc,cd->dij/dot_general | solution.py:172
  452.1 7.0 copy.31
  459.1 76.8 %all-to-all-done.3 = bf16[128,144,128]{2,1,0:T(8,128)(2,1)} async-done(((bf16[128,144,128]{2,1,0:T(8,128)(2,1)}), bf16[128,144,128]{2,1,0:T(8,128)(2,1)}, u32[]{:S(2)}, u32[]{:S(2)}) %all-to-all-start.3) | async-done | bytes 4718624 | tf_op jit(solution)/shard_map/all_to_all | solution.py:161
  535.9 109.2 %all_to_all.32 = bf16[128,144,128]{2,1,0:T(8,128)(2,1)} all-to-all(bf16[128,144,128]{2,1,0:T(8,128)(2,1)} %copy.31), channel_id=1, replica_groups=mesh['row'=8,'col'=4] {'row','col'}, dimensions={0} | all-to-all | bytes 9437184 | tf_op jit(solution)/shard_map/all_to_all | solution.py:161
  645.1 8.8 %triangle_in.1 = bf16[8,4,4,144,128]{4,3,2,1,0:T(8,128)(2,1)S(1)} custom-call(bf16[8,4,4,144,128]{4,3,2,1,0:T(8,128)(2,1)} %bitcast.30.left_ref, bf16[8,4,4,144,128]{4,3,2,1,0:T(8,128)(2,1)} %bitcast.97), custom_call_target="tpu_custom_call" | custom-call | flops 3623878656 | bytes 14155776 | tf_op jit(solution)/shard_map/triangle_in/pallas_call | solution.py:118
  653.9 0.0 copy-start.15
  653.9 0.0 copy-start.16
  653.9 108.3 %all_to_all.33 = bf16[128,144,128]{2,1,0:T(8,128)(2,1)S(1)} all-to-all(bf16[128,144,128]{2,1,0:T(8,128)(2,1)S(1)} %bitcast.91), channel_id=1, replica_groups=mesh['row'=8,'col'=4] {'row','col'}, dimensions={0} | all-to-all | bytes 9437184 | tf_op jit(solution)/shard_map/all_to_all | solution.py:161
  762.2 0.7 convert_reduce_fusion.2
  762.9 1.3 fusion.16
  764.2 0.0 copy-done.15
  764.2 0.0 copy-done.16
  764.3 0.0 slice-start.2
  764.3 2.2 fusion.19
  766.5 0.0 slice-start.3
  766.5 1.4 fusion.26
  767.9 0.7 slice-done.3
  768.6 9.1 %fusion.25 = bf16[144,128,128]{2,1,0:T(8,128)(2,1)S(1)} fusion(bf16[144,128,128]{2,1,0:T(8,128)(2,1)S(1)} %bitcast.95, f32[144,128,128]{2,1,0:T(8,128)S(1)} %fusion.26, bf16[128,640]{1,0:T(8,128)(2,1)S(1)} %copy-done.5, f32[128]{0:T(128)S(1)} %get-tuple-element.14, f32[128]{0:T(128)S(1)} %get-tuple-element.17, f32[144,128]{1,0:T(8,128)S(1)} %add_rsqrt_fusion.1, ...), kind=kOutput, calls=%fused_computation.35 | convolution fusion | flops 634650624 | bytes 23774208 | tf_op jit(solution)/shard_map/ijc,cd->ijd/dot_general | solution.py:193
  777.8 0.1 slice.125
  777.9 0.4 slice.124
  778.3 0.1 copy.33
  778.4 2.6 pad_maximum_fusion.1
  (52 shorter events, 0.3 us)
Async XLA Ops:
  0.0 7.3 copy-start.4
  7.3 11.1 %copy-start.6 = (f32[96,128,1]{1,0,2:T(8,128)S(1)}, f32[96,128,1]{1,0,2:T(8,128)}, u32[]{:S(2)}) copy-start(f32[96,128,1]{1,0,2:T(8,128)} %slice.113) | copy-start | bytes 147460
  7.9 15.5 %copy-start.7 = (bf16[128,640]{1,0:T(8,128)(2,1)}, bf16[128,640]{1,0:T(8,128)(2,1)S(1)}, u32[]{:S(2)}) copy-start(bf16[128,640]{1,0:T(8,128)(2,1)S(1)} %get-tuple-element.6) | copy-start | bytes 491524
  9.6 13.9 %copy-start.1 = (bf16[2,48,64,128]{3,2,0,1:T(8,128)(2,1)}, bf16[2,48,64,128]{3,2,0,1:T(8,128)(2,1)S(1)}, u32[]{:S(2)}) copy-start(bf16[2,48,64,128]{3,2,0,1:T(8,128)(2,1)S(1)} %copy.25) | copy-start | bytes 4718596
  16.9 42.4 %copy-start.11 = (f32[144,128]{1,0:T(8,128)}, f32[144,128]{1,0:T(8,128)S(1)}, u32[]{:S(2)}) copy-start(f32[144,128]{1,0:T(8,128)S(1)} %add_rsqrt_fusion.3) | copy-start | bytes 221188
  18.4 41.0 %copy-start.17 = (f32[128]{0:T(128)}, f32[128]{0:T(128)S(1)}, u32[]{:S(2)}) copy-start(f32[128]{0:T(128)S(1)} %get-tuple-element.13) | copy-start | bytes 1540
  18.4 41.0 %copy-start.19 = (f32[128]{0:T(128)}, f32[128]{0:T(128)S(1)}, u32[]{:S(2)}) copy-start(f32[128]{0:T(128)S(1)} %get-tuple-element.18) | copy-start | bytes 1540
  18.4 41.0 %copy-start.9 = (f32[144,128]{1,0:T(8,128)}, f32[144,128]{1,0:T(8,128)S(1)}, u32[]{:S(2)}) copy-start(f32[144,128]{1,0:T(8,128)S(1)} %maximum_bitcast_fusion) | copy-start | bytes 221188
  36.9 14.5 %copy-start.8 = (bf16[128,640]{1,0:T(8,128)(2,1)S(1)}, bf16[128,640]{1,0:T(8,128)(2,1)}, u32[]{:S(2)}) copy-start(bf16[128,640]{1,0:T(8,128)(2,1)} %copy-done.7) | copy-start | bytes 491524
  43.9 112.5 %all-to-all-start = ((bf16[128,144,128]{2,1,0:T(8,128)(2,1)}), bf16[128,144,128]{2,1,0:T(8,128)(2,1)}, u32[]{:S(2)}, u32[]{:S(2)}) async-start(bf16[128,144,128]{2,1,0:T(8,128)(2,1)} %copy.27), calls=%async_computation | async-start | bytes 9437184 | tf_op jit(solution)/shard_map/all_to_all | solution.py:161
  51.4 8.0 %copy-start.2 = (bf16[2,48,64,128]{3,2,0,1:T(8,128)(2,1)S(1)}, bf16[2,48,64,128]{3,2,0,1:T(8,128)(2,1)}, u32[]{:S(2)}) copy-start(bf16[2,48,64,128]{3,2,0,1:T(8,128)(2,1)} %copy-done.1) | copy-start | bytes 4718596
  382.2 4.2 copy-start.13
  386.4 1.5 copy-start.3
  386.5 1.5 copy-start.12
  386.5 1.5 copy-start.18
  386.5 1.5 copy-start.20
  388.0 16.0 %copy-start.5 = (bf16[128,640]{1,0:T(8,128)(2,1)S(1)}, bf16[128,640]{1,0:T(8,128)(2,1)}, u32[]{:S(2)}) copy-start(bf16[128,640]{1,0:T(8,128)(2,1)} %get-tuple-element.5) | copy-start | bytes 491524
  398.4 10.6 %copy-start = (bf16[144,128,128]{2,1,0:T(8,128)(2,1)}, bf16[144,128,128]{2,1,0:T(8,128)(2,1)S(1)}, u32[]{:S(2)}) copy-start(bf16[144,128,128]{2,1,0:T(8,128)(2,1)S(1)} %get-tuple-element.16) | copy-start | bytes 14155780
  403.9 5.1 copy-start.10
  426.8 14.5 %slice-start = ((s8[4718592]{0:T(1024)(128)(4,1)}), s8[524288]{0:T(1024)(128)(4,1)S(1)}, s32[]{:S(2)}) async-start(s8[4718592]{0:T(1024)(128)(4,1)} %bitcast.92), calls=%async_computation.6 | async-start | bytes 1048576
  426.8 109.1 %all-to-all-start.3 = ((bf16[128,144,128]{2,1,0:T(8,128)(2,1)}), bf16[128,144,128]{2,1,0:T(8,128)(2,1)}, u32[]{:S(2)}, u32[]{:S(2)}) async-start(bf16[128,144,128]{2,1,0:T(8,128)(2,1)} %copy.30), calls=%async_computation.3 | async-start | bytes 9437184 | tf_op jit(solution)/shard_map/all_to_all | solution.py:161
  430.7 10.6 %slice-start.1 = ((s8[4718592]{0:T(1024)(128)(4,1)}), s8[4194304]{0:T(1024)(128)(4,1)S(1)}, s32[]{:S(2)}) async-start(s8[4718592]{0:T(1024)(128)(4,1)} %bitcast.92), calls=%async_computation.7 | async-start | bytes 8388608
  653.9 110.3 %copy-start.15 = (f32[128]{0:T(128)S(1)}, f32[128]{0:T(128)}, u32[]{:S(2)}) copy-start(f32[128]{0:T(128)} %get-tuple-element.11) | copy-start | bytes 1540
  653.9 110.3 %copy-start.16 = (f32[128]{0:T(128)S(1)}, f32[128]{0:T(128)}, u32[]{:S(2)}) copy-start(f32[128]{0:T(128)} %get-tuple-element.20) | copy-start | bytes 1540
  762.2 4.2 copy-start.14
  764.3 3.6 slice-start.2
  766.5 2.2 slice-start.3

commit v2 on v1

--- a/solution.py
+++ b/solution.py
@@ -48,16 +48,20 @@
     return jnp.concatenate([first[:, lanes], second[:, lanes]], axis=1)
 
 
-def triangle_kernel(geometry, incoming, left_ref, right_ref, out_ref, left, right, tri):
-    n_row, n_col, rows, cols = geometry
+def triangle_kernel(geometry, incoming, *refs):
+    n_row, n_col, rows, cols, first_rows = geometry
     half = rows // 2
-
-    def unpack(source, target, packed_rows):
+    left_parts, right_parts, out_parts = refs[0:2], refs[2:4], refs[4:6]
+    left, right, tri = refs[6:]
+    rest = rows - first_rows
+
+    def runs_of(r, packed_rows):
+        return segments(r * rows, rows, cols, n_col) if packed_rows else [(0, r * rows, rows)]
+
+    def unpack(parts, target, packed_rows):
+        first, second = parts
         for r in range(n_row):
-            if packed_rows:
-                runs = segments(r * rows, rows, cols, n_col)
-            else:
-                runs = [(0, r * rows, rows)]
+            runs = runs_of(r, packed_rows)
 
             def put(offset, block, lane_at):
                 size = block.shape[0]
@@ -69,66 +73,71 @@
                         )
 
             for s in range(n_col):
-                put(0, source[r, s, 0, :rows, :], s * LANES)
+                put(0, first[r, s, 0], s * LANES)
+                put(first_rows, second[r, s, 0, :rest, :], s * LANES)
             for p in range(n_col // 2):
-                first = source[r, 2 * p, 0, rows:, :]
-                second = source[r, 2 * p + 1, 0, rows:, :]
+                even = second[r, 2 * p, 0, rest:, :]
+                odd = second[r, 2 * p + 1, 0, rest:, :]
                 lane_at = (n_col + p) * LANES
-                put(0, join(first, second, False), lane_at)
-                put(half, join(first, second, True), lane_at)
-
-    unpack(left_ref, left, False)
-    unpack(right_ref, right, not incoming)
+                put(0, join(even, odd, False), lane_at)
+                put(half, join(even, odd, True), lane_at)
+
+    unpack(left_parts, left, False)
+    unpack(right_parts, right, not incoming)
     contract = ((0,), (0,)) if incoming else ((1,), (1,))
     tri[...] = lax.dot_general(
         left[...], right[...], (contract, ((), ())), preferred_element_type=jnp.float32
     ).astype(tri.dtype)
 
+    first, second = out_parts
     for r in range(n_row):
-        if incoming:
-            runs = segments(r * rows, rows, cols, n_col)
-        else:
-            runs = [(0, r * rows, rows)]
+        runs = runs_of(r, incoming)
 
         def get(offset, size, lane_at):
-            parts = []
+            pieces = []
             for begin, packed, length in runs:
                 lo, hi = max(begin, offset), min(begin + length, offset + size)
                 if lo < hi:
-                    parts.append(
+                    pieces.append(
                         tri[packed + lo - begin:packed + hi - begin, lane_at:lane_at + LANES]
                     )
-            return parts[0] if len(parts) == 1 else jnp.concatenate(parts, axis=0)
+            return pieces[0] if len(pieces) == 1 else jnp.concatenate(pieces, axis=0)
 
         for s in range(n_col):
-            out_ref[r, s, 0, :rows, :] = get(0, rows, s * LANES)
+            first[r, s, 0] = get(0, first_rows, s * LANES)
+            second[r, s, 0, :rest, :] = get(first_rows, rest, s * LANES)
         for p in range(n_col // 2):
             lane_at = (n_col + p) * LANES
             above, below = get(0, half, lane_at), get(half, half, lane_at)
-            out_ref[r, 2 * p, 0, rows:, :] = join(above, below, False)
-            out_ref[r, 2 * p + 1, 0, rows:, :] = join(above, below, True)
+            second[r, 2 * p, 0, rest:, :] = join(above, below, False)
+            second[r, 2 * p + 1, 0, rest:, :] = join(above, below, True)
 
 
 def triangle(left, right, geometry, incoming):
-    n_row, n_col, rows, cols = geometry
-    owned, packed, lanes = left.shape[0] // (n_row * n_col), left.shape[1], left.shape[2]
+    n_row, n_col, rows = geometry[:3]
+    owned = left[0].shape[0] // (n_row * n_col)
     total = n_row * rows
-    shape = (n_row, n_col, owned, packed, lanes)
-    spec = pl.BlockSpec((n_row, n_col, 1, packed, lanes), lambda c: (0, 0, c, 0, 0))
-    out = pl.pallas_call(
+    shapes = [(n_row, n_col, owned) + part.shape[1:] for part in left]
+    specs = [
+        pl.BlockSpec((n_row, n_col, 1) + shape[3:], lambda c: (0, 0, c, 0, 0)) for shape in shapes
+    ]
+    outs = pl.pallas_call(
         functools.partial(triangle_kernel, geometry, incoming),
         grid=(owned,),
-        in_specs=[spec, spec],
-        out_specs=spec,
-        out_shape=jax.ShapeDtypeStruct(shape, jnp.bfloat16),
+        in_specs=specs * 2,
+        out_specs=specs,
+        out_shape=[jax.ShapeDtypeStruct(shape, jnp.bfloat16) for shape in shapes],
         scratch_shapes=[pltpu.VMEM((total, total), jnp.bfloat16)] * 3,
         cost_estimate=pl.CostEstimate(
-            flops=2 * owned * total**3, bytes_accessed=6 * left.size, transcendentals=0
+            flops=2 * owned * total**3,
+            bytes_accessed=6 * sum(part.size for part in left),
+            transcendentals=0,
         ),
         compiler_params=pltpu.CompilerParams(vmem_limit_bytes=48 * 2**20),
         name="triangle_in" if incoming else "triangle_out",
-    )(left.reshape(shape), right.reshape(shape))
-    return out.reshape(left.shape)
+    )(*[part.reshape(shape) for part, shape in zip(left, shapes)],
+      *[part.reshape(shape) for part, shape in zip(right, shapes)])
+    return [out.reshape(part.shape) for out, part in zip(outs, left)]
 
 
 def pack_tile(tile):
@@ -147,7 +156,8 @@
     tile_rows, tile_cols, channels = pair.shape
     n_row = lax.axis_size("row")
     n_col = lax.axis_size("col")
-    geometry = (n_row, n_col, tile_rows, tile_cols)
+    first_rows = tile_rows - 16
+    geometry = (n_row, n_col, tile_rows, tile_cols, first_rows)
     total = n_row * tile_rows
     row_index = lax.axis_index("row") * tile_rows + jnp.arange(tile_rows, dtype=jnp.int32)
     col_index = lax.axis_index("col") * tile_cols + jnp.arange(tile_cols, dtype=jnp.int32)
@@ -156,49 +166,59 @@
         * live_values(col_index, chain_lengths, total)[None, :]
     )
     pmask = pack_tile(pmask[:, :, None])[:, :, 0]
+    masks = [pmask[:first_rows], pmask[first_rows:]]
 
     def exchange(block):
         return lax.all_to_all(block, ("row", "col"), split_axis=0, concat_axis=0, tiled=True)
 
-    state = pack_tile(pair)
+    def factor(normed, weights_in, column_block, mask):
+        def project(at):
+            block = weights_in[:, at * channels : (at + 1) * channels]
+            return jnp.einsum("ijc,cd->dij", normed, block, preferred_element_type=jnp.float32)
+
+        gate = jax.nn.sigmoid(project(column_block + 1))
+        return (mask[None] * gate * project(column_block)).astype(jnp.bfloat16)
+
+    states = [
+        pair[:first_rows, :LANES],
+        jnp.concatenate(
+            [
+                pair[first_rows:, :LANES],
+                pair[:, LANES:].reshape(2, tile_rows // 2, HALF, channels)
+                .transpose(1, 0, 2, 3)
+                .reshape(tile_rows // 2, LANES, channels),
+            ],
+            axis=0,
+        ),
+    ]
     for update_index in range(2):
         weights_in = w_in[update_index]
-        normed = layer_norm(state, gains[update_index, 0], biases[update_index, 0], 2).astype(
-            jnp.bfloat16
-        )
-
-        def project_first(column_block):
-            block = weights_in[:, column_block * channels : (column_block + 1) * channels]
-            return jnp.einsum("ijc,cd->dij", normed, block, preferred_element_type=jnp.float32)
-
-        left_edges = (pmask[None] * jax.nn.sigmoid(project_first(1)) * project_first(0)).astype(
-            jnp.bfloat16
-        )
-        right_edges = (pmask[None] * jax.nn.sigmoid(project_first(3)) * project_first(2)).astype(
-            jnp.bfloat16
-        )
-        products = triangle(
-            exchange(left_edges), exchange(right_edges), geometry, update_index == 1
-        )
-        returned = exchange(products)
-        gain_out = gains[update_index, 1]
-        bias_out = biases[update_index, 1]
-        normed_out = layer_norm(
-            returned, gain_out[:, None, None], bias_out[:, None, None], 0
-        ).astype(jnp.bfloat16)
-        mixed = jnp.einsum(
-            "cij,cd->ijd", normed_out, w_out[update_index], preferred_element_type=jnp.float32
-        )
-        gate_vals = jax.nn.sigmoid(
-            jnp.einsum(
-                "ijc,cd->ijd",
-                normed,
-                weights_in[:, 4 * channels : 5 * channels],
-                preferred_element_type=jnp.float32,
-            )
-        )
-        state = (state.astype(jnp.float32) + gate_vals * mixed).astype(jnp.bfloat16)
-    return unpack_tile(state, tile_rows)
+        gain_in, gain_out = gains[update_index, 0], gains[update_index, 1]
+        bias_in, bias_out = biases[update_index, 0], biases[update_index, 1]
+        normed = [layer_norm(state, gain_in, bias_in, 2).astype(jnp.bfloat16) for state in states]
+        left = [exchange(factor(n, weights_in, 0, m)) for n, m in zip(normed, masks)]
+        right = [exchange(factor(n, weights_in, 2, m)) for n, m in zip(normed, masks)]
+        products = triangle(left, right, geometry, update_index == 1)
+        later = []
+        for state, normed_part, part in zip(states, normed, products):
+            returned = exchange(part)
+            normed_out = layer_norm(
+                returned, gain_out[:, None, None], bias_out[:, None, None], 0
+            ).astype(jnp.bfloat16)
+            mixed = jnp.einsum(
+                "cij,cd->ijd", normed_out, w_out[update_index], preferred_element_type=jnp.float32
+            )
+            gate_vals = jax.nn.sigmoid(
+                jnp.einsum(
+                    "ijc,cd->ijd",
+                    normed_part,
+                    weights_in[:, 4 * channels : 5 * channels],
+                    preferred_element_type=jnp.float32,
+                )
+            )
+            later.append((state.astype(jnp.float32) + gate_vals * mixed).astype(jnp.bfloat16))
+        states = later
+    return unpack_tile(jnp.concatenate(states, axis=0), tile_rows)
 
 
 def body(pair, chain_lengths, gains, biases, w_in, w_out):

time: 782 us -> 768 us (0.982); the launches traced: 781 us -> 758 us
  blocking collectives: 435 us -> 233 us
  waiting for transfers between devices: 153 us -> 276 us
  starting transfers between devices: 11.4 us -> 36.1 us
  matrix products: 99.4 us -> 116 us
  other arithmetic: 25.4 us -> 34.5 us
    all_to_all x4, blocking collectives: 435 us -> 233 us  [exchange(): lax.all_to_all(block, ('row', 'col'), split_axis=0, concat_axis=0, tiled=...]
    all_to_all x2 -> x8, waiting for transfers between devices: 153 us -> 276 us  [exchange(): lax.all_to_all(block, ('row', 'col'), split_axis=0, concat_axis=0, tiled=...]
    all_to_all x2 -> x8, starting transfers between devices: 11.4 us -> 36.1 us  [exchange(): lax.all_to_all(block, ('row', 'col'), split_axis=0, concat_axis=0, tiled=...]
    dot_general x10 -> x20, matrix products: 96.6 us -> 105 us  [the longest x16 83.1 us: project(): jnp.einsum('ijc,cd->dij', normed, block, preferred_element_type=jnp.float32)]
    dot_general x2 -> x4, matrix products: 2.86 us -> 11.1 us  [packed_body(): jnp.einsum('cij,cd->ijd', normed_out, w_out[update_index], preferred_elem...]
    convert_element_type x4 -> x8, local copies, waits for them, and re-layouts: 28 us -> 35.3 us  [factor(): return (mask[None] * gate * project(column_block)).astype(jnp.bfloat16)]
    reduce_sum x4 -> x8, other arithmetic: 14 us -> 15.7 us  [layer_norm(): variance = jnp.mean(centred * centred, axis=axis_pos, keepdims=True)]
  transfers between devices with their start and end apart: 2 -> 8, of which waited for: 2 -> 8; matrix products, arithmetic and copies ran while one was open for 7% -> 21% of each run, Pallas kernels for 0% -> 0%
where the time goes in v2:
time: 768 us; the launch traced here: 758 us
  waiting for transfers between devices  276 us (36%)
  blocking collectives  233 us (30%)
  matrix products  116 us (15%)
  local copies, waits for them, and re-layouts  43.6 us (6%)
  starting transfers between devices  36.1 us (5%)
  other arithmetic  34.5 us (4%)
  Pallas kernels  17.8 us (2%)
    all_to_all x8, waiting for transfers between devices, exchange(): lax.all_to_all(block, ('row', 'col'), split_axis=0, concat_axis=0, tiled=...  276 us
    all_to_all x4, blocking collectives, exchange(): lax.all_to_all(block, ('row', 'col'), split_axis=0, concat_axis=0, tiled=...  233 us
    dot_general x16, matrix products, project(): jnp.einsum('ijc,cd->dij', normed, block, preferred_element_type=jnp.float32)  83.1 us
    all_to_all x8, starting transfers between devices, exchange(): lax.all_to_all(block, ('row', 'col'), split_axis=0, concat_axis=0, tiled=...  36.1 us
    convert_element_type x8, local copies, waits for them, and re-layouts, factor(): return (mask[None] * gate * project(column_block)).astype(jnp.bfloat16)  35.3 us
    dot_general x4, matrix products, packed_body(): jnp.einsum('ijc,cd->ijd', normed_part, weights_in[:, 4 * channels:5 * cha...  22.2 us
    pallas_call x2, Pallas kernels, triangle(): pl.pallas_call(functools.partial(triangle_kernel, geometry, incoming), gr...  17.8 us
    reduce_sum x8, other arithmetic, layer_norm(): variance = jnp.mean(centred * centred, axis=axis_pos, keepdims=True)  15.7 us
  transfers between devices with their start and end apart: 8, of which 8 were waited for; matrix products, arithmetic and copies ran while one was open for 21% of the time, Pallas kernels for 0%

profile of v2, /device:TPU:0, one launch (start us, length us, event | category | flops | bytes accessed | tf_op | source)
XLA Modules:
  0.0 758.1 jit_solution(3030238270080579286)
XLA Ops:
  0.0 2.0 slice.120
  2.6 2.1 convert_reduce_fusion.5
  4.7 2.6 fusion.39
  8.6 2.4 fusion.79
  11.0 5.3 fusion.64
  16.3 4.1 copy.42
  20.4 7.5 all-to-all-start.3
  27.8 2.4 fusion.77
  30.2 5.3 fusion.63
  35.5 4.1 copy.40
  39.7 36.9 %all-to-all-done.3 = bf16[128,64,128]{2,1,0:T(8,128)(2,1)} async-done(((bf16[128,64,128]{2,1,0:T(8,128)(2,1)}), bf16[128,64,128]{2,1,0:T(8,128)(2,1)}, u32[]{:S(2)}, u32[]{:S(2)}) %all-to-all-start.3) | async-done | bytes 2097184 | tf_op jit(solution)/shard_map/all_to_all | solution.py:172
  76.6 4.1 all-to-all-start.1
  80.7 2.5 convert_reduce_fusion.1
  83.2 4.8 fusion.12
  88.1 6.7 fusion.80
  94.8 6.6 fusion.58
  101.4 4.7 copy.41
  106.1 23.3 %all-to-all-done.1 = bf16[128,64,128]{2,1,0:T(8,128)(2,1)S(1)} async-done(((bf16[128,64,128]{2,1,0:T(8,128)(2,1)}), bf16[128,64,128]{2,1,0:T(8,128)(2,1)S(1)}, u32[]{:S(2)}, u32[]{:S(2)}) %all-to-all-start.1) | async-done | bytes 2097184 | tf_op jit(solution)/shard_map/all_to_all | solution.py:172
  129.4 4.4 all-to-all-start.2
  133.8 6.7 fusion.78
  140.5 7.0 fusion.57
  147.5 4.7 copy.37
  152.2 41.6 %all-to-all-done.2 = bf16[128,80,128]{2,1,0:T(8,128)(2,1)} async-done(((bf16[128,80,128]{2,1,0:T(8,128)(2,1)}), bf16[128,80,128]{2,1,0:T(8,128)(2,1)}, u32[]{:S(2)}, u32[]{:S(2)}) %all-to-all-start.2) | async-done | bytes 2621472 | tf_op jit(solution)/shard_map/all_to_all | solution.py:172
  193.8 64.7 %all_to_all.60 = bf16[128,80,128]{2,1,0:T(8,128)(2,1)} all-to-all(bf16[128,80,128]{2,1,0:T(8,128)(2,1)} %copy.37), channel_id=1, replica_groups=mesh['row'=8,'col'=4] {'row','col'}, dimensions={0} | all-to-all | bytes 5242880 | tf_op jit(solution)/shard_map/all_to_all | solution.py:172
  258.6 8.5 %triangle_out.1 = (bf16[8,4,4,80,128]{4,3,2,1,0:T(8,128)(2,1)}, bf16[8,4,4,64,128]{4,3,2,1,0:T(8,128)(2,1)S(1)}) custom-call(bf16[8,4,4,80,128]{4,3,2,1,0:T(8,128)(2,1)} %bitcast.143, bf16[8,4,4,64,128]{4,3,2,1,0:T(8,128)(2,1)S(1)} %bitcast.123, bf16[8,4,4,80,128]{4,3,2,1,0:T(8,128)(2,1)} %bitcast.20.refs_2_, bf16[8,4,4,64,128]{4,3,2,1,0:T(8,128)(2,1)} %bitcast.22.refs_3_), custom_call_target="tpu_custom_call" | custom-call | flops 3623878656 | bytes 14155776 | tf_op jit(solution)/shard_map/triangle_out/pallas_call | solution.py:124
  267.1 51.6 %all_to_all.61 = bf16[128,64,128]{2,1,0:T(8,128)(2,1)} all-to-all(bf16[128,64,128]{2,1,0:T(8,128)(2,1)S(1)} %bitcast.124), channel_id=1, replica_groups=mesh['row'=8,'col'=4] {'row','col'}, dimensions={0} | all-to-all | bytes 4194304 | tf_op jit(solution)/shard_map/all_to_all | solution.py:172
  318.7 3.7 all-to-all-start.4
  322.4 6.3 fusion.76
  330.6 6.3 convert_reduce_fusion.4
  336.9 2.4 fusion.35
  339.3 2.4 fusion.84
  341.7 5.5 fusion.66
  347.1 4.2 copy.48
  351.3 31.1 %all-to-all-done.4 = bf16[128,80,128]{2,1,0:T(8,128)(2,1)S(1)} async-done(((bf16[128,80,128]{2,1,0:T(8,128)(2,1)}), bf16[128,80,128]{2,1,0:T(8,128)(2,1)S(1)}, u32[]{:S(2)}, u32[]{:S(2)}) %all-to-all-start.4) | async-done | bytes 2621472 | tf_op jit(solution)/shard_map/all_to_all | solution.py:172
  382.4 4.6 all-to-all-start.9
  387.0 4.5 fusion.82
  391.6 5.5 fusion.65
  397.0 4.2 copy.46
  402.3 33.4 %all-to-all-done.9 = bf16[128,64,128]{2,1,0:T(8,128)(2,1)} async-done(((bf16[128,64,128]{2,1,0:T(8,128)(2,1)}), bf16[128,64,128]{2,1,0:T(8,128)(2,1)}, u32[]{:S(2)}, u32[]{:S(2)}) %all-to-all-start.9) | async-done | bytes 2097184 | tf_op jit(solution)/shard_map/all_to_all | solution.py:172
  435.7 4.1 all-to-all-start.7
  439.8 2.9 fusion.23
  443.6 1.3 slice-done.3
  444.9 6.4 convert_reduce_fusion
  451.3 3.3 fusion.8
  454.6 2.9 fusion.85
  457.5 6.6 fusion.60
  464.1 4.7 copy.47
  468.8 19.7 %all-to-all-done.7 = bf16[128,64,128]{2,1,0:T(8,128)(2,1)S(1)} async-done(((bf16[128,64,128]{2,1,0:T(8,128)(2,1)}), bf16[128,64,128]{2,1,0:T(8,128)(2,1)S(1)}, u32[]{:S(2)}, u32[]{:S(2)}) %all-to-all-start.7) | async-done | bytes 2097184 | tf_op jit(solution)/shard_map/all_to_all | solution.py:172
  488.5 4.2 all-to-all-start.8
  492.8 6.8 fusion.83
  499.6 6.7 fusion.59
  506.3 4.7 copy.44
  511.0 41.9 %all-to-all-done.8 = bf16[128,80,128]{2,1,0:T(8,128)(2,1)} async-done(((bf16[128,80,128]{2,1,0:T(8,128)(2,1)}), bf16[128,80,128]{2,1,0:T(8,128)(2,1)}, u32[]{:S(2)}, u32[]{:S(2)}) %all-to-all-start.8) | async-done | bytes 2621472 | tf_op jit(solution)/shard_map/all_to_all | solution.py:172
  552.8 64.9 %all_to_all.62 = bf16[128,80,128]{2,1,0:T(8,128)(2,1)} all-to-all(bf16[128,80,128]{2,1,0:T(8,128)(2,1)} %copy.44), channel_id=1, replica_groups=mesh['row'=8,'col'=4] {'row','col'}, dimensions={0} | all-to-all | bytes 5242880 | tf_op jit(solution)/shard_map/all_to_all | solution.py:172
  617.7 9.3 %triangle_in.1 = (bf16[8,4,4,80,128]{4,3,2,1,0:T(8,128)(2,1)}, bf16[8,4,4,64,128]{4,3,2,1,0:T(8,128)(2,1)S(1)}) custom-call(bf16[8,4,4,80,128]{4,3,2,1,0:T(8,128)(2,1)} %bitcast.144, bf16[8,4,4,64,128]{4,3,2,1,0:T(8,128)(2,1)S(1)} %bitcast.122, bf16[8,4,4,80,128]{4,3,2,1,0:T(8,128)(2,1)} %bitcast.42.refs_2_, bf16[8,4,4,64,128]{4,3,2,1,0:T(8,128)(2,1)} %bitcast.44.refs_3_), custom_call_target="tpu_custom_call" | custom-call | flops 3623878656 | bytes 14155776 | tf_op jit(solution)/shard_map/triangle_in/pallas_call | solution.py:124
  627.0 51.6 %all_to_all.63 = bf16[128,64,128]{2,1,0:T(8,128)(2,1)} all-to-all(bf16[128,64,128]{2,1,0:T(8,128)(2,1)S(1)} %bitcast.125), channel_id=1, replica_groups=mesh['row'=8,'col'=4] {'row','col'}, dimensions={0} | all-to-all | bytes 4194304 | tf_op jit(solution)/shard_map/all_to_all | solution.py:172
  678.6 3.7 all-to-all-start.10
  682.3 4.5 fusion.81
  688.7 3.1 fusion.52
  692.0 1.2 copy-done.11
  693.1 1.3 copy.51
  694.5 47.9 %all-to-all-done.10 = bf16[128,80,128]{2,1,0:T(8,128)(2,1)S(1)} async-done(((bf16[128,80,128]{2,1,0:T(8,128)(2,1)}), bf16[128,80,128]{2,1,0:T(8,128)(2,1)S(1)}, u32[]{:S(2)}, u32[]{:S(2)}) %all-to-all-start.10) | async-done | bytes 2621472 | tf_op jit(solution)/shard_map/all_to_all | solution.py:172
  746.4 5.0 fusion.25
  751.4 6.4 fusion.34
  (118 shorter events, 11.8 us)
Async XLA Ops:
  0.0 2.4 slice-start.4
  0.0 2.0 copy-start.24
  2.2 2.6 copy-start.14
  2.4 6.1 copy-start.22
  2.4 6.1 copy-start.23
  2.6 27.6 %copy-start.9 = (bf16[2,48,64,128]{3,2,0,1:T(8,128)(2,1)}, bf16[2,48,64,128]{3,2,0,1:T(8,128)(2,1)S(1)}, u32[]{:S(2)}) copy-start(bf16[2,48,64,128]{3,2,0,1:T(8,128)(2,1)S(1)} %copy.39) | copy-start | bytes 4718596
  2.6 6.0 copy-start.15
  7.4 22.9 %copy-start.20 = (f32[64,128]{1,0:T(8,128)}, f32[64,128]{1,0:T(8,128)S(1)}, u32[]{:S(2)}) copy-start(f32[64,128]{1,0:T(8,128)S(1)} %add_rsqrt_fusion.7) | copy-start | bytes 98308
  8.4 132.1 %copy-start.16 = (bf16[128,640]{1,0:T(8,128)(2,1)}, bf16[128,640]{1,0:T(8,128)(2,1)S(1)}, u32[]{:S(2)}) copy-start(bf16[128,640]{1,0:T(8,128)(2,1)S(1)} %get-tuple-element.14) | copy-start | bytes 491524
  8.6 131.9 %copy-start.25 = (f32[128]{0:T(128)}, f32[128]{0:T(128)S(1)}, u32[]{:S(2)}) copy-start(f32[128]{0:T(128)S(1)} %get-tuple-element.21) | copy-start | bytes 1540
  8.6 131.9 %copy-start.28 = (f32[128]{0:T(128)}, f32[128]{0:T(128)S(1)}, u32[]{:S(2)}) copy-start(f32[128]{0:T(128)S(1)} %get-tuple-element.28) | copy-start | bytes 1540
  8.6 21.6 %copy-start.18 = (f32[64,128]{1,0:T(8,128)}, f32[64,128]{1,0:T(8,128)S(1)}, u32[]{:S(2)}) copy-start(f32[64,128]{1,0:T(8,128)S(1)} %fusion.67) | copy-start | bytes 98308
  20.4 56.2 %all-to-all-start.3 = ((bf16[128,64,128]{2,1,0:T(8,128)(2,1)}), bf16[128,64,128]{2,1,0:T(8,128)(2,1)}, u32[]{:S(2)}, u32[]{:S(2)}) async-start(bf16[128,64,128]{2,1,0:T(8,128)(2,1)} %copy.42), calls=%async_computation.3 | async-start | bytes 4194304 | tf_op jit(solution)/shard_map/all_to_all | solution.py:172
  76.6 52.8 %all-to-all-start.1 = ((bf16[128,64,128]{2,1,0:T(8,128)(2,1)}), bf16[128,64,128]{2,1,0:T(8,128)(2,1)S(1)}, u32[]{:S(2)}, u32[]{:S(2)}) async-start(bf16[128,64,128]{2,1,0:T(8,128)(2,1)} %copy.40), calls=%async_computation.1 | async-start | bytes 4194304 | tf_op jit(solution)/shard_map/all_to_all | solution.py:172
  83.2 11.6 %slice-start = ((s8[4718592]{0:T(1024)(128)(4,1)}), s8[4194304]{0:T(1024)(128)(4,1)S(1)}, s32[]{:S(2)}) async-start(s8[4718592]{0:T(1024)(128)(4,1)} %bitcast.134), calls=%async_computation.12 | async-start | bytes 8388608
  88.1 6.7 slice-start.1
  129.4 64.4 %all-to-all-start.2 = ((bf16[128,80,128]{2,1,0:T(8,128)(2,1)}), bf16[128,80,128]{2,1,0:T(8,128)(2,1)}, u32[]{:S(2)}, u32[]{:S(2)}) async-start(bf16[128,80,128]{2,1,0:T(8,128)(2,1)} %copy.41), calls=%async_computation.2 | async-start | bytes 5242880 | tf_op jit(solution)/shard_map/all_to_all | solution.py:172
  267.1 55.3 %copy-start.21 = (f32[64,128]{1,0:T(8,128)S(1)}, f32[64,128]{1,0:T(8,128)}, u32[]{:S(2)}) copy-start(f32[64,128]{1,0:T(8,128)} %copy-done.20) | copy-start | bytes 98308
  267.1 55.3 %copy-start.26 = (f32[128]{0:T(128)S(1)}, f32[128]{0:T(128)}, u32[]{:S(2)}) copy-start(f32[128]{0:T(128)} %copy-done.25) | copy-start | bytes 1540
  267.1 55.3 %copy-start.29 = (f32[128]{0:T(128)S(1)}, f32[128]{0:T(128)}, u32[]{:S(2)}) copy-start(f32[128]{0:T(128)} %copy-done.28) | copy-start | bytes 1540
  318.7 63.7 %all-to-all-start.4 = ((bf16[128,80,128]{2,1,0:T(8,128)(2,1)}), bf16[128,80,128]{2,1,0:T(8,128)(2,1)S(1)}, u32[]{:S(2)}, u32[]{:S(2)}) async-start(bf16[128,80,128]{2,1,0:T(8,128)(2,1)} %bitcast.141), calls=%async_computation.4 | async-start | bytes 5242880 | tf_op jit(solution)/shard_map/all_to_all | solution.py:172
  322.4 6.3 copy-start.5
  328.7 1.9 copy-start.10
  328.7 1.9 copy-start.17
  336.8 4.8 copy-start.1
  336.9 4.8 copy-start.19
  382.4 19.2 %copy-start = (bf16[128,80,128]{2,1,0:T(8,128)(2,1)}, bf16[128,80,128]{2,1,0:T(8,128)(2,1)S(1)}, u32[]{:S(2)}) copy-start(bf16[128,80,128]{2,1,0:T(8,128)(2,1)S(1)} %all-to-all-done.4) | copy-start | bytes 7864324
  382.4 53.3 %all-to-all-start.9 = ((bf16[128,64,128]{2,1,0:T(8,128)(2,1)}), bf16[128,64,128]{2,1,0:T(8,128)(2,1)}, u32[]{:S(2)}, u32[]{:S(2)}) async-start(bf16[128,64,128]{2,1,0:T(8,128)(2,1)} %copy.48), calls=%async_computation.9 | async-start | bytes 4194304 | tf_op jit(solution)/shard_map/all_to_all | solution.py:172
  387.0 4.5 copy-start.2
  435.7 52.8 %all-to-all-start.7 = ((bf16[128,64,128]{2,1,0:T(8,128)(2,1)}), bf16[128,64,128]{2,1,0:T(8,128)(2,1)S(1)}, u32[]{:S(2)}, u32[]{:S(2)}) async-start(bf16[128,64,128]{2,1,0:T(8,128)(2,1)} %copy.46), calls=%async_computation.7 | async-start | bytes 4194304 | tf_op jit(solution)/shard_map/all_to_all | solution.py:172
  439.8 3.8 slice-start.2
  442.7 2.2 slice-start.3
  442.7 2.2 copy-start.27
  442.7 2.2 copy-start.30
  451.3 6.2 copy-start.6
  488.5 64.3 %all-to-all-start.8 = ((bf16[128,80,128]{2,1,0:T(8,128)(2,1)}), bf16[128,80,128]{2,1,0:T(8,128)(2,1)}, u32[]{:S(2)}, u32[]{:S(2)}) async-start(bf16[128,80,128]{2,1,0:T(8,128)(2,1)} %copy.47), calls=%async_computation.8 | async-start | bytes 5242880 | tf_op jit(solution)/shard_map/all_to_all | solution.py:172
  492.8 6.8 copy-start.7
  678.6 63.7 %all-to-all-start.10 = ((bf16[128,80,128]{2,1,0:T(8,128)(2,1)}), bf16[128,80,128]{2,1,0:T(8,128)(2,1)S(1)}, u32[]{:S(2)}, u32[]{:S(2)}) async-start(bf16[128,80,128]{2,1,0:T(8,128)(2,1)} %bitcast.142), calls=%async_computation.10 | async-start | bytes 5242880 | tf_op jit(solution)/shard_map/all_to_all | solution.py:172
  682.3 4.5 copy-start.4
  686.9 1.9 copy-start.3
  691.8 1.3 copy-start.11
  744.6 1.7 copy-start.8
  746.4 5.0 copy-start.12
  746.4 5.1 copy-start.13

commit v3 on v2

--- a/solution.py
+++ b/solution.py
@@ -51,9 +51,15 @@
 def triangle_kernel(geometry, incoming, *refs):
     n_row, n_col, rows, cols, first_rows = geometry
     half = rows // 2
-    left_parts, right_parts, out_parts = refs[0:2], refs[2:4], refs[4:6]
-    left, right, tri = refs[6:]
+    left_first, others, first_out, second_out = refs[:4]
+    left, right, tri = refs[4:]
     rest = rows - first_rows
+    second_rows = rest + half
+    left_parts = (left_first, others.at[:, :, :, :second_rows])
+    right_parts = (
+        others.at[:, :, :, second_rows:second_rows + first_rows],
+        others.at[:, :, :, second_rows + first_rows:],
+    )
 
     def runs_of(r, packed_rows):
         return segments(r * rows, rows, cols, n_col) if packed_rows else [(0, r * rows, rows)]
@@ -85,11 +91,18 @@
     unpack(left_parts, left, False)
     unpack(right_parts, right, not incoming)
     contract = ((0,), (0,)) if incoming else ((1,), (1,))
-    tri[...] = lax.dot_general(
-        left[...], right[...], (contract, ((), ())), preferred_element_type=jnp.float32
-    ).astype(tri.dtype)
-
-    first, second = out_parts
+    total = tri.shape[0]
+    block = 2 * LANES if total % (2 * LANES) == 0 else LANES
+
+    @pl.loop(0, total // block)
+    def _(at):
+        span = pl.ds(pl.multiple_of(at * block, block), block)
+        lhs = left[:, span] if incoming else left[span, :]
+        tri[span, :] = lax.dot_general(
+            lhs, right[...], (contract, ((), ())), preferred_element_type=jnp.float32
+        ).astype(tri.dtype)
+
+    first, second = first_out, second_out
     for r in range(n_row):
         runs = runs_of(r, incoming)
 
@@ -113,31 +126,36 @@
             second[r, 2 * p + 1, 0, rest:, :] = join(above, below, True)
 
 
-def triangle(left, right, geometry, incoming):
-    n_row, n_col, rows = geometry[:3]
-    owned = left[0].shape[0] // (n_row * n_col)
+def triangle(left_first, others, geometry, incoming):
+    n_row, n_col, rows, _, first_rows = geometry
+    devices = n_row * n_col
+    owned, lanes = left_first.shape[0] // devices, left_first.shape[2]
     total = n_row * rows
-    shapes = [(n_row, n_col, owned) + part.shape[1:] for part in left]
-    specs = [
-        pl.BlockSpec((n_row, n_col, 1) + shape[3:], lambda c: (0, 0, c, 0, 0)) for shape in shapes
-    ]
+    second_rows = rows + rows // 2 - first_rows
+
+    def shape_of(length):
+        return (n_row, n_col, owned, length, lanes)
+
+    def spec_of(length):
+        return pl.BlockSpec((n_row, n_col, 1, length, lanes), lambda c: (0, 0, c, 0, 0))
+
+    lengths_in, lengths_out = (first_rows, others.shape[1]), (first_rows, second_rows)
     outs = pl.pallas_call(
         functools.partial(triangle_kernel, geometry, incoming),
         grid=(owned,),
-        in_specs=specs * 2,
-        out_specs=specs,
-        out_shape=[jax.ShapeDtypeStruct(shape, jnp.bfloat16) for shape in shapes],
+        in_specs=[spec_of(length) for length in lengths_in],
+        out_specs=[spec_of(length) for length in lengths_out],
+        out_shape=[jax.ShapeDtypeStruct(shape_of(length), jnp.bfloat16) for length in lengths_out],
         scratch_shapes=[pltpu.VMEM((total, total), jnp.bfloat16)] * 3,
         cost_estimate=pl.CostEstimate(
             flops=2 * owned * total**3,
-            bytes_accessed=6 * sum(part.size for part in left),
+            bytes_accessed=3 * (left_first.size + others.size),
             transcendentals=0,
         ),
         compiler_params=pltpu.CompilerParams(vmem_limit_bytes=48 * 2**20),
         name="triangle_in" if incoming else "triangle_out",
-    )(*[part.reshape(shape) for part, shape in zip(left, shapes)],
-      *[part.reshape(shape) for part, shape in zip(right, shapes)])
-    return [out.reshape(part.shape) for out, part in zip(outs, left)]
+    )(left_first.reshape(shape_of(lengths_in[0])), others.reshape(shape_of(lengths_in[1])))
+    return [out.reshape(devices * owned, out.shape[3], lanes) for out in outs]
 
 
 def pack_tile(tile):
@@ -196,12 +214,15 @@
         gain_in, gain_out = gains[update_index, 0], gains[update_index, 1]
         bias_in, bias_out = biases[update_index, 0], biases[update_index, 1]
         normed = [layer_norm(state, gain_in, bias_in, 2).astype(jnp.bfloat16) for state in states]
-        left = [exchange(factor(n, weights_in, 0, m)) for n, m in zip(normed, masks)]
-        right = [exchange(factor(n, weights_in, 2, m)) for n, m in zip(normed, masks)]
-        products = triangle(left, right, geometry, update_index == 1)
+        left = [factor(n, weights_in, 0, m) for n, m in zip(normed, masks)]
+        right = [factor(n, weights_in, 2, m) for n, m in zip(normed, masks)]
+        left_first = exchange(left[0])
+        others = jnp.concatenate([left[1], right[0], right[1]], axis=1)
+        products = triangle(left_first, exchange(others), geometry, update_index == 1)
+        returned_first = exchange(products[0])
+        returned_first, second = lax.optimization_barrier((returned_first, products[1]))
         later = []
-        for state, normed_part, part in zip(states, normed, products):
-            returned = exchange(part)
+        for state, normed_part, returned in zip(states, normed, (returned_first, exchange(second))):
             normed_out = layer_norm(
                 returned, gain_out[:, None, None], bias_out[:, None, None], 0
             ).astype(jnp.bfloat16)

time: 768 us -> 745 us (0.970)
  blocking collectives: 233 us -> 373 us
  waiting for transfers between devices: 276 us -> 136 us
  matrix products: 116 us -> 96.1 us
  other arithmetic: 34.5 us -> 49.8 us
  starting transfers between devices: 36.1 us -> 23.2 us
  local copies, waits for them, and re-layouts: 43.6 us -> 35.1 us
    all_to_all x4 -> x3, blocking collectives: 233 us -> 373 us  [exchange(): lax.all_to_all(block, ('row', 'col'), split_axis=0, concat_axis=0, tiled=...]
    all_to_all x8 -> x5, waiting for transfers between devices: 276 us -> 136 us  [exchange(): lax.all_to_all(block, ('row', 'col'), split_axis=0, concat_axis=0, tiled=...]
    convert_element_type x8 -> x2, local copies, waits for them, and re-layouts: 35.3 us -> 7.89 us  [factor(): return (mask[None] * gate * project(column_block)).astype(jnp.bfloat16)]
    dot_general x16, matrix products: 83.1 us -> 62.5 us  [project(): jnp.einsum('ijc,cd->dij', normed, block, preferred_element_type=jnp.float32)]
    concatenate x0 -> x2, local copies, waits for them, and re-layouts: none -> 20.2 us  [packed_body(): others = jnp.concatenate([left[1], right[0], right[1]], axis=1)]
    all_to_all x8 -> x5, starting transfers between devices: 36.1 us -> 23.2 us  [exchange(): lax.all_to_all(block, ('row', 'col'), split_axis=0, concat_axis=0, tiled=...]
  transfers between devices with their start and end apart: 8 -> 5, of which waited for: 8 -> 5; matrix products, arithmetic and copies ran while one was open for 21% -> 19% of each run, Pallas kernels for 0% -> 0%
where the time goes in v3:
time: 745 us; the launch traced here: 739 us
  blocking collectives  373 us (50%)
  waiting for transfers between devices  136 us (18%)
  matrix products  96.1 us (13%)
  other arithmetic  49.8 us (7%)
  local copies, waits for them, and re-layouts  35.1 us (5%)
  Pallas kernels  24.4 us (3%)
  starting transfers between devices  23.2 us (3%)
    all_to_all x3, blocking collectives, exchange(): lax.all_to_all(block, ('row', 'col'), split_axis=0, concat_axis=0, tiled=...  373 us
    all_to_all x5, waiting for transfers between devices, exchange(): lax.all_to_all(block, ('row', 'col'), split_axis=0, concat_axis=0, tiled=...  136 us
    dot_general x16, matrix products, project(): jnp.einsum('ijc,cd->dij', normed, block, preferred_element_type=jnp.float32)  62.5 us
    pallas_call x2, Pallas kernels, triangle(): pl.pallas_call(functools.partial(triangle_kernel, geometry, incoming), gr...  24.4 us
    all_to_all x5, starting transfers between devices, exchange(): lax.all_to_all(block, ('row', 'col'), split_axis=0, concat_axis=0, tiled=...  23.2 us
    dot_general x4, matrix products, packed_body(): jnp.einsum('ijc,cd->ijd', normed_part, weights_in[:, 4 * channels:5 * cha...  22.5 us
    concatenate x2, local copies, waits for them, and re-layouts, packed_body(): others = jnp.concatenate([left[1], right[0], right[1]], axis=1)  20.2 us
    reduce_sum x8, other arithmetic, layer_norm(): variance = jnp.mean(centred * centred, axis=axis_pos, keepdims=True)  18.9 us
  transfers between devices with their start and end apart: 5, of which 5 were waited for; matrix products, arithmetic and copies ran while one was open for 19% of the time, Pallas kernels for 0%

profile of v3, /device:TPU:0, one launch (start us, length us, event | category | flops | bytes accessed | tf_op | source)
XLA Modules:
  0.0 739.0 jit_solution(6346047246044743559)
XLA Ops:
  0.0 1.1 slice_bitcast_fusion
  1.9 0.9 select_reduce_fusion.1
  2.8 2.7 convert_reduce_fusion.1
  5.6 4.7 fusion.12
  11.1 2.9 fusion.78
  14.0 5.2 fusion.57
  19.2 3.2 copy.29
  22.4 8.0 %all-to-all-start = ((bf16[128,80,128]{2,1,0:T(8,128)(2,1)}), bf16[128,80,128]{2,1,0:T(8,128)(2,1)}, u32[]{:S(2)}, u32[]{:S(2)}) async-start(bf16[128,80,128]{2,1,0:T(8,128)(2,1)} %copy.29), calls=%async_computation | async-start | bytes 5242880 | tf_op jit(solution)/shard_map/all_to_all | solution.py:190
  30.4 1.1 slice.120
  32.3 2.6 fusion.39
  35.2 4.2 fusion.77
  39.5 2.4 fusion.79
  41.8 2.9 fusion.80
  44.7 4.0 fusion.63
  48.7 4.0 fusion.64
  52.7 5.1 fusion.58
  57.9 3.5 pad_maximum_fusion
  61.4 9.9 %copy.32 = bf16[128,208,128]{2,1,0:T(8,128)(2,1)} copy(bf16[128,208,128]{0,2,1:T(8,128)(2,1)} %pad_maximum_fusion) | data formatting | bytes 13631488 | tf_op jit(solution)/shard_map/concatenate | solution.py:220
  71.3 19.1 %all-to-all-done = bf16[128,80,128]{2,1,0:T(8,128)(2,1)} async-done(((bf16[128,80,128]{2,1,0:T(8,128)(2,1)}), bf16[128,80,128]{2,1,0:T(8,128)(2,1)}, u32[]{:S(2)}, u32[]{:S(2)}) %all-to-all-start) | async-done | bytes 2621472 | tf_op jit(solution)/shard_map/all_to_all | solution.py:190
  90.4 154.6 %all_to_all.40 = bf16[128,208,128]{2,1,0:T(8,128)(2,1)} all-to-all(bf16[128,208,128]{2,1,0:T(8,128)(2,1)} %copy.32), channel_id=1, replica_groups=mesh['row'=8,'col'=4] {'row','col'}, dimensions={0} | all-to-all | bytes 13631488 | tf_op jit(solution)/shard_map/all_to_all | solution.py:190
  245.1 12.1 %triangle_out.1 = (bf16[8,4,4,80,128]{4,3,2,1,0:T(8,128)(2,1)}, bf16[8,4,4,64,128]{4,3,2,1,0:T(8,128)(2,1)}) custom-call(bf16[8,4,4,80,128]{4,3,2,1,0:T(8,128)(2,1)} %bitcast.8.refs_0_, bf16[8,4,4,208,128]{4,3,2,1,0:T(8,128)(2,1)} %bitcast.132), custom_call_target="tpu_custom_call" | custom-call | flops 3623878656 | bytes 14155776 | tf_op jit(solution)/shard_map/triangle_out/pallas_call | solution.py:143
  257.2 3.1 all-to-all-start.2
  260.3 5.1 fusion.76
  265.4 55.0 %all-to-all-done.2 = bf16[128,80,128]{2,1,0:T(8,128)(2,1)S(1)} async-done(((bf16[128,80,128]{2,1,0:T(8,128)(2,1)}), bf16[128,80,128]{2,1,0:T(8,128)(2,1)S(1)}, u32[]{:S(2)}, u32[]{:S(2)}) %all-to-all-start.2) | async-done | bytes 2621472 | tf_op jit(solution)/shard_map/all_to_all | solution.py:190
  320.3 4.4 all-to-all-start.4
  325.9 1.1 fusion.23
  327.1 0.9 fusion.55
  328.0 1.3 slice-done.3
  329.3 6.4 convert_reduce_fusion
  335.7 3.3 fusion.8
  339.0 2.9 fusion.83
  341.9 6.7 fusion.59
  348.6 4.7 copy.34
  353.2 2.9 fusion.85
  356.1 6.7 fusion.60
  362.8 10.6 %all-to-all-done.4 = bf16[128,64,128]{2,1,0:T(8,128)(2,1)} async-done(((bf16[128,64,128]{2,1,0:T(8,128)(2,1)}), bf16[128,64,128]{2,1,0:T(8,128)(2,1)}, u32[]{:S(2)}, u32[]{:S(2)}) %all-to-all-start.4) | async-done | bytes 2097184 | tf_op jit(solution)/shard_map/all_to_all | solution.py:190
  373.4 4.3 all-to-all-start.3
  377.8 2.1 convert_reduce_fusion.7
  379.9 2.4 fusion.47
  382.3 2.5 fusion.50
  384.8 6.3 convert_reduce_fusion.4
  391.1 2.4 fusion.35
  393.5 2.4 fusion.82
  395.9 2.4 fusion.84
  398.2 4.0 fusion.65
  402.2 4.0 fusion.66
  406.2 3.5 pad_maximum_fusion.1
  409.7 10.3 %copy.36 = bf16[128,208,128]{2,1,0:T(8,128)(2,1)} copy(bf16[128,208,128]{0,2,1:T(8,128)(2,1)} %pad_maximum_fusion.1) | data formatting | bytes 13631488 | tf_op jit(solution)/shard_map/concatenate | solution.py:220
  420.0 17.8 %all-to-all-done.3 = bf16[128,80,128]{2,1,0:T(8,128)(2,1)S(1)} async-done(((bf16[128,80,128]{2,1,0:T(8,128)(2,1)}), bf16[128,80,128]{2,1,0:T(8,128)(2,1)S(1)}, u32[]{:S(2)}, u32[]{:S(2)}) %all-to-all-start.3) | async-done | bytes 2621472 | tf_op jit(solution)/shard_map/all_to_all | solution.py:190
  437.8 155.0 %all_to_all.41 = bf16[128,208,128]{2,1,0:T(8,128)(2,1)} all-to-all(bf16[128,208,128]{2,1,0:T(8,128)(2,1)} %copy.36), channel_id=1, replica_groups=mesh['row'=8,'col'=4] {'row','col'}, dimensions={0} | all-to-all | bytes 13631488 | tf_op jit(solution)/shard_map/all_to_all | solution.py:190
  592.8 12.2 %triangle_in.1 = (bf16[8,4,4,80,128]{4,3,2,1,0:T(8,128)(2,1)S(1)}, bf16[8,4,4,64,128]{4,3,2,1,0:T(8,128)(2,1)}) custom-call(bf16[8,4,4,80,128]{4,3,2,1,0:T(8,128)(2,1)} %bitcast.136, bf16[8,4,4,208,128]{4,3,2,1,0:T(8,128)(2,1)} %bitcast.133), custom_call_target="tpu_custom_call" | custom-call | flops 3623878656 | bytes 14155776 | tf_op jit(solution)/shard_map/triangle_in/pallas_call | solution.py:143
  605.0 63.4 %all_to_all.42 = bf16[128,80,128]{2,1,0:T(8,128)(2,1)S(1)} all-to-all(bf16[128,80,128]{2,1,0:T(8,128)(2,1)S(1)} %bitcast.118), channel_id=1, replica_groups=mesh['row'=8,'col'=4] {'row','col'}, dimensions={0} | all-to-all | bytes 5242880 | tf_op jit(solution)/shard_map/all_to_all | solution.py:190
  668.4 3.5 all-to-all-start.7
  671.9 5.1 fusion.81
  678.3 1.1 fusion.19
  679.4 0.9 fusion.53
  681.1 5.9 fusion.25
  687.0 33.7 %all-to-all-done.7 = bf16[128,64,128]{2,1,0:T(8,128)(2,1)} async-done(((bf16[128,64,128]{2,1,0:T(8,128)(2,1)}), bf16[128,64,128]{2,1,0:T(8,128)(2,1)}, u32[]{:S(2)}, u32[]{:S(2)}) %all-to-all-start.7) | async-done | bytes 2097184 | tf_op jit(solution)/shard_map/all_to_all | solution.py:190
  720.7 2.1 convert_reduce_fusion.6
  722.8 2.2 fusion.43
  725.0 2.5 fusion.46
  727.5 3.1 fusion.52
  730.9 1.5 copy-done.12
  732.4 6.4 fusion.34
  (129 shorter events, 6.2 us)
Async XLA Ops:
  0.0 10.4 %copy-start.30 = (f32[2,2,128]{2,1,0:T(2,128)S(1)}, f32[2,2,128]{2,1,0:T(2,128)}, u32[]{:S(2)}) copy-start(f32[2,2,128]{2,1,0:T(2,128)} %param.8) | copy-start | bytes 6148
  0.0 10.4 %copy-start.29 = (f32[2,2,128]{2,1,0:T(2,128)S(1)}, f32[2,2,128]{2,1,0:T(2,128)}, u32[]{:S(2)}) copy-start(f32[2,2,128]{2,1,0:T(2,128)} %param.9) | copy-start | bytes 6148
  1.1 12.9 %copy-start.14 = (bf16[128,640]{1,0:T(8,128)(2,1)}, bf16[128,640]{1,0:T(8,128)(2,1)S(1)}, u32[]{:S(2)}) copy-start(bf16[128,640]{1,0:T(8,128)(2,1)S(1)} %get-tuple-element.22) | copy-start | bytes 491524
  1.9 9.2 %copy-start.6 = (bf16[96,192,128]{2,1,0:T(8,128)(2,1)S(1)}, bf16[96,192,128]{2,1,0:T(8,128)(2,1)}, u32[]{:S(2)}) copy-start(bf16[96,192,128]{2,1,0:T(8,128)(2,1)} %param.6) | copy-start | bytes 14155780
  10.3 3.7 copy-start.17
  10.4 21.1 %copy-start.13 = (f32[96,192,1]{1,0,2:T(8,128)}, f32[96,192,1]{1,0,2:T(8,128)S(1)}, u32[]{:S(2)}) copy-start(f32[96,192,1]{1,0,2:T(8,128)S(1)} %broadcast_multiply_fusion) | copy-start | bytes 221188
  11.0 2.9 copy-start.31
  11.0 2.9 copy-start.35
  22.4 9.1 %slice-start.4 = ((bf16[96,192,128]{2,1,0:T(8,128)(2,1)}), bf16[96,64,128]{2,1,0:T(8,128)(2,1)S(1)}, s32[]{:S(2)}) async-start(bf16[96,192,128]{2,1,0:T(8,128)(2,1)} %param.6), calls=%async_computation.12 | async-start | bytes 3145728 | tf_op jit(solution)/shard_map/slice | solution.py:205
  22.4 68.0 %all-to-all-start = ((bf16[128,80,128]{2,1,0:T(8,128)(2,1)}), bf16[128,80,128]{2,1,0:T(8,128)(2,1)}, u32[]{:S(2)}, u32[]{:S(2)}) async-start(bf16[128,80,128]{2,1,0:T(8,128)(2,1)} %copy.29), calls=%async_computation | async-start | bytes 5242880 | tf_op jit(solution)/shard_map/all_to_all | solution.py:190
  31.5 0.9 copy-start.7
  31.5 3.5 slice-start.5
  31.5 3.6 slice-start.6
  31.7 17.0 %copy-start.4 = (bf16[2,48,64,128]{3,2,0,1:T(8,128)(2,1)}, bf16[2,48,64,128]{3,2,0,1:T(8,128)(2,1)S(1)}, u32[]{:S(2)}) copy-start(bf16[2,48,64,128]{3,2,0,1:T(8,128)(2,1)S(1)} %copy.31) | copy-start | bytes 4718596
  34.9 4.5 copy-start.8
  34.9 4.5 copy-start.15
  35.0 4.5 copy-start.32
  35.0 4.5 copy-start.36
  35.1 13.6 %copy-start.19 = (f32[64,128]{1,0:T(8,128)}, f32[64,128]{1,0:T(8,128)S(1)}, u32[]{:S(2)}) copy-start(f32[64,128]{1,0:T(8,128)S(1)} %fusion.67) | copy-start | bytes 98308
  35.1 6.7 slice-start
  39.4 2.4 slice-start.1
  39.4 2.4 copy-start.18
  257.2 3.1 copy-start.33
  257.2 3.1 copy-start.37
  257.2 63.1 %all-to-all-start.2 = ((bf16[128,80,128]{2,1,0:T(8,128)(2,1)}), bf16[128,80,128]{2,1,0:T(8,128)(2,1)S(1)}, u32[]{:S(2)}, u32[]{:S(2)}) async-start(bf16[128,80,128]{2,1,0:T(8,128)(2,1)} %bitcast.21), calls=%async_computation.2 | async-start | bytes 5242880 | tf_op jit(solution)/shard_map/all_to_all | solution.py:190
  320.3 5.6 copy-start.27
  320.3 5.6 copy-start.28
  320.3 53.1 %all-to-all-start.4 = ((bf16[128,64,128]{2,1,0:T(8,128)(2,1)}), bf16[128,64,128]{2,1,0:T(8,128)(2,1)}, u32[]{:S(2)}, u32[]{:S(2)}) async-start(bf16[128,64,128]{2,1,0:T(8,128)(2,1)} %bitcast.22), calls=%async_computation.4 | async-start | bytes 4194304 | tf_op jit(solution)/shard_map/all_to_all | solution.py:190
  325.1 1.9 copy-start.16
  325.9 2.0 slice-start.2
  327.0 2.2 slice-start.3
  327.1 2.2 copy-start.34
  327.1 2.2 copy-start.38
  329.2 9.7 %copy-start.21 = (f32[128]{0:T(128)S(1)}, f32[128]{0:T(128)}, u32[]{:S(2)}) copy-start(f32[128]{0:T(128)} %get-tuple-element.30) | copy-start | bytes 1540
  329.2 9.7 %copy-start.23 = (f32[128]{0:T(128)S(1)}, f32[128]{0:T(128)}, u32[]{:S(2)}) copy-start(f32[128]{0:T(128)} %get-tuple-element.35) | copy-start | bytes 1540
  335.6 20.5 %copy-start.2 = (bf16[80,128,128]{2,1,0:T(8,128)(2,1)}, bf16[80,128,128]{2,1,0:T(8,128)(2,1)S(1)}, u32[]{:S(2)}) copy-start(bf16[80,128,128]{2,1,0:T(8,128)(2,1)S(1)} %get-tuple-element.34) | copy-start | bytes 7864324
  373.4 64.4 %all-to-all-start.3 = ((bf16[128,80,128]{2,1,0:T(8,128)(2,1)}), bf16[128,80,128]{2,1,0:T(8,128)(2,1)S(1)}, u32[]{:S(2)}, u32[]{:S(2)}) async-start(bf16[128,80,128]{2,1,0:T(8,128)(2,1)} %copy.34), calls=%async_computation.3 | async-start | bytes 5242880 | tf_op jit(solution)/shard_map/all_to_all | solution.py:190
  377.7 7.0 copy-start.5
  377.7 7.0 copy-start.39
  384.7 8.7 %copy-start.22 = (f32[128]{0:T(128)S(1)}, f32[128]{0:T(128)}, u32[]{:S(2)}) copy-start(f32[128]{0:T(128)} %get-tuple-element.30) | copy-start | bytes 1540
  384.8 8.7 %copy-start.24 = (f32[128]{0:T(128)S(1)}, f32[128]{0:T(128)}, u32[]{:S(2)}) copy-start(f32[128]{0:T(128)} %get-tuple-element.35) | copy-start | bytes 1540
  391.0 11.2 %copy-start = (bf16[64,128,128]{2,1,0:T(8,128)(2,1)}, bf16[64,128,128]{2,1,0:T(8,128)(2,1)S(1)}, u32[]{:S(2)}) copy-start(bf16[64,128,128]{2,1,0:T(8,128)(2,1)S(1)} %get-tuple-element.32) | copy-start | bytes 6291460
  395.9 2.4 copy-start.20
  402.2 4.0 copy-start.11
  437.8 155.0 %copy-start.10 = (bf16[128,80,128]{2,1,0:T(8,128)(2,1)}, bf16[128,80,128]{2,1,0:T(8,128)(2,1)S(1)}, u32[]{:S(2)}) copy-start(bf16[128,80,128]{2,1,0:T(8,128)(2,1)S(1)} %all-to-all-done.3) | copy-start | bytes 7864324
  668.4 52.3 %all-to-all-start.7 = ((bf16[128,64,128]{2,1,0:T(8,128)(2,1)}), bf16[128,64,128]{2,1,0:T(8,128)(2,1)}, u32[]{:S(2)}, u32[]{:S(2)}) async-start(bf16[128,64,128]{2,1,0:T(8,128)(2,1)} %bitcast.42), calls=%async_computation.7 | async-start | bytes 4194304 | tf_op jit(solution)/shard_map/all_to_all | solution.py:190
  677.1 1.2 copy-start.25
  677.1 1.2 copy-start.26
  679.4 1.7 copy-start.3
  687.0 40.5 %copy-start.1 = (bf16[64,128,128]{2,1,0:T(8,128)(2,1)S(1)}, bf16[64,128,128]{2,1,0:T(8,128)(2,1)}, u32[]{:S(2)}) copy-start(bf16[64,128,128]{2,1,0:T(8,128)(2,1)} %copy-done) | copy-start | bytes 6291460
  720.7 6.8 copy-start.9
  730.7 1.7 copy-start.12

commit v4 on v3

--- a/solution.py
+++ b/solution.py
@@ -91,16 +91,9 @@
     unpack(left_parts, left, False)
     unpack(right_parts, right, not incoming)
     contract = ((0,), (0,)) if incoming else ((1,), (1,))
-    total = tri.shape[0]
-    block = 2 * LANES if total % (2 * LANES) == 0 else LANES
-
-    @pl.loop(0, total // block)
-    def _(at):
-        span = pl.ds(pl.multiple_of(at * block, block), block)
-        lhs = left[:, span] if incoming else left[span, :]
-        tri[span, :] = lax.dot_general(
-            lhs, right[...], (contract, ((), ())), preferred_element_type=jnp.float32
-        ).astype(tri.dtype)
+    tri[...] = lax.dot_general(
+        left[...], right[...], (contract, ((), ())), preferred_element_type=jnp.float32
+    ).astype(tri.dtype)
 
     first, second = first_out, second_out
     for r in range(n_row):

time: 745 us -> 739 us (level)
  no operation moved by 1% of the time
where the time goes in v4:
time: 739 us; the launch traced here: 734 us
  blocking collectives  373 us (50%)
  waiting for transfers between devices  136 us (18%)
  matrix products  96.1 us (13%)
  other arithmetic  49.8 us (7%)
  local copies, waits for them, and re-layouts  35.1 us (5%)
  starting transfers between devices  23.2 us (3%)
  Pallas kernels  19 us (3%)
    all_to_all x3, blocking collectives, exchange(): lax.all_to_all(block, ('row', 'col'), split_axis=0, concat_axis=0, tiled=...  373 us
    all_to_all x5, waiting for transfers between devices, exchange(): lax.all_to_all(block, ('row', 'col'), split_axis=0, concat_axis=0, tiled=...  136 us
    dot_general x16, matrix products, project(): jnp.einsum('ijc,cd->dij', normed, block, preferred_element_type=jnp.float32)  62.5 us
    all_to_all x5, starting transfers between devices, exchange(): lax.all_to_all(block, ('row', 'col'), split_axis=0, concat_axis=0, tiled=...  23.2 us
    dot_general x4, matrix products, packed_body(): jnp.einsum('ijc,cd->ijd', normed_part, weights_in[:, 4 * channels:5 * cha...  22.5 us
    concatenate x2, local copies, waits for them, and re-layouts, packed_body(): others = jnp.concatenate([left[1], right[0], right[1]], axis=1)  20.2 us
    pallas_call x2, Pallas kernels, triangle(): pl.pallas_call(functools.partial(triangle_kernel, geometry, incoming), gr...  19 us
    reduce_sum x8, other arithmetic, layer_norm(): variance = jnp.mean(centred * centred, axis=axis_pos, keepdims=True)  18.9 us
  transfers between devices with their start and end apart: 5, of which 5 were waited for; matrix products, arithmetic and copies ran while one was open for 19% of the time, Pallas kernels for 0%

profile of v4, /device:TPU:0, one launch (start us, length us, event | category | flops | bytes accessed | tf_op | source)
XLA Modules:
  0.0 733.6 jit_solution(4312130999073093805)
XLA Ops:
  0.0 1.1 slice_bitcast_fusion
  1.9 0.9 select_reduce_fusion.1
  2.8 2.7 convert_reduce_fusion.1
  5.6 4.7 fusion.12
  11.1 2.9 fusion.78
  14.0 5.2 fusion.57
  19.2 3.2 copy.29
  22.4 8.0 %all-to-all-start = ((bf16[128,80,128]{2,1,0:T(8,128)(2,1)}), bf16[128,80,128]{2,1,0:T(8,128)(2,1)}, u32[]{:S(2)}, u32[]{:S(2)}) async-start(bf16[128,80,128]{2,1,0:T(8,128)(2,1)} %copy.29), calls=%async_computation | async-start | bytes 5242880 | tf_op jit(solution)/shard_map/all_to_all | solution.py:183
  30.4 1.1 slice.120
  32.3 2.6 fusion.39
  35.2 4.2 fusion.77
  39.5 2.4 fusion.79
  41.8 2.9 fusion.80
  44.7 4.0 fusion.63
  48.7 4.0 fusion.64
  52.7 5.1 fusion.58
  57.9 3.5 pad_maximum_fusion
  61.4 9.9 %copy.32 = bf16[128,208,128]{2,1,0:T(8,128)(2,1)} copy(bf16[128,208,128]{0,2,1:T(8,128)(2,1)} %pad_maximum_fusion) | data formatting | bytes 13631488 | tf_op jit(solution)/shard_map/concatenate | solution.py:213
  71.3 19.1 %all-to-all-done = bf16[128,80,128]{2,1,0:T(8,128)(2,1)} async-done(((bf16[128,80,128]{2,1,0:T(8,128)(2,1)}), bf16[128,80,128]{2,1,0:T(8,128)(2,1)}, u32[]{:S(2)}, u32[]{:S(2)}) %all-to-all-start) | async-done | bytes 2621472 | tf_op jit(solution)/shard_map/all_to_all | solution.py:183
  90.4 154.6 %all_to_all.40 = bf16[128,208,128]{2,1,0:T(8,128)(2,1)} all-to-all(bf16[128,208,128]{2,1,0:T(8,128)(2,1)} %copy.32), channel_id=1, replica_groups=mesh['row'=8,'col'=4] {'row','col'}, dimensions={0} | all-to-all | bytes 13631488 | tf_op jit(solution)/shard_map/all_to_all | solution.py:183
  245.1 9.4 %triangle_out.1 = (bf16[8,4,4,80,128]{4,3,2,1,0:T(8,128)(2,1)}, bf16[8,4,4,64,128]{4,3,2,1,0:T(8,128)(2,1)}) custom-call(bf16[8,4,4,80,128]{4,3,2,1,0:T(8,128)(2,1)} %bitcast.8.refs_0_, bf16[8,4,4,208,128]{4,3,2,1,0:T(8,128)(2,1)} %bitcast.132), custom_call_target="tpu_custom_call" | custom-call | flops 3623878656 | bytes 14155776 | tf_op jit(solution)/shard_map/triangle_out/pallas_call | solution.py:136
  254.5 3.1 all-to-all-start.2
  257.6 5.1 fusion.76
  262.7 55.0 %all-to-all-done.2 = bf16[128,80,128]{2,1,0:T(8,128)(2,1)S(1)} async-done(((bf16[128,80,128]{2,1,0:T(8,128)(2,1)}), bf16[128,80,128]{2,1,0:T(8,128)(2,1)S(1)}, u32[]{:S(2)}, u32[]{:S(2)}) %all-to-all-start.2) | async-done | bytes 2621472 | tf_op jit(solution)/shard_map/all_to_all | solution.py:183
  317.6 4.4 all-to-all-start.4
  323.2 1.1 fusion.23
  324.4 0.9 fusion.55
  325.3 1.3 slice-done.3
  326.5 6.4 convert_reduce_fusion
  332.9 3.3 fusion.8
  336.3 2.9 fusion.83
  339.2 6.7 fusion.59
  345.8 4.7 copy.34
  350.5 2.9 fusion.85
  353.4 6.7 fusion.60
  360.1 10.6 %all-to-all-done.4 = bf16[128,64,128]{2,1,0:T(8,128)(2,1)} async-done(((bf16[128,64,128]{2,1,0:T(8,128)(2,1)}), bf16[128,64,128]{2,1,0:T(8,128)(2,1)}, u32[]{:S(2)}, u32[]{:S(2)}) %all-to-all-start.4) | async-done | bytes 2097184 | tf_op jit(solution)/shard_map/all_to_all | solution.py:183
  370.7 4.3 all-to-all-start.3
  375.0 2.1 convert_reduce_fusion.7
  377.2 2.4 fusion.47
  379.6 2.5 fusion.50
  382.1 6.3 convert_reduce_fusion.4
  388.3 2.4 fusion.35
  390.8 2.4 fusion.82
  393.2 2.4 fusion.84
  395.5 4.0 fusion.65
  399.5 4.0 fusion.66
  403.5 3.5 pad_maximum_fusion.1
  407.0 10.3 %copy.36 = bf16[128,208,128]{2,1,0:T(8,128)(2,1)} copy(bf16[128,208,128]{0,2,1:T(8,128)(2,1)} %pad_maximum_fusion.1) | data formatting | bytes 13631488 | tf_op jit(solution)/shard_map/concatenate | solution.py:213
  417.3 17.8 %all-to-all-done.3 = bf16[128,80,128]{2,1,0:T(8,128)(2,1)S(1)} async-done(((bf16[128,80,128]{2,1,0:T(8,128)(2,1)}), bf16[128,80,128]{2,1,0:T(8,128)(2,1)S(1)}, u32[]{:S(2)}, u32[]{:S(2)}) %all-to-all-start.3) | async-done | bytes 2621472 | tf_op jit(solution)/shard_map/all_to_all | solution.py:183
  435.1 155.0 %all_to_all.41 = bf16[128,208,128]{2,1,0:T(8,128)(2,1)} all-to-all(bf16[128,208,128]{2,1,0:T(8,128)(2,1)} %copy.36), channel_id=1, replica_groups=mesh['row'=8,'col'=4] {'row','col'}, dimensions={0} | all-to-all | bytes 13631488 | tf_op jit(solution)/shard_map/all_to_all | solution.py:183
  590.1 9.5 %triangle_in.1 = (bf16[8,4,4,80,128]{4,3,2,1,0:T(8,128)(2,1)S(1)}, bf16[8,4,4,64,128]{4,3,2,1,0:T(8,128)(2,1)}) custom-call(bf16[8,4,4,80,128]{4,3,2,1,0:T(8,128)(2,1)} %bitcast.136, bf16[8,4,4,208,128]{4,3,2,1,0:T(8,128)(2,1)} %bitcast.133), custom_call_target="tpu_custom_call" | custom-call | flops 3623878656 | bytes 14155776 | tf_op jit(solution)/shard_map/triangle_in/pallas_call | solution.py:136
  599.6 63.4 %all_to_all.42 = bf16[128,80,128]{2,1,0:T(8,128)(2,1)S(1)} all-to-all(bf16[128,80,128]{2,1,0:T(8,128)(2,1)S(1)} %bitcast.118), channel_id=1, replica_groups=mesh['row'=8,'col'=4] {'row','col'}, dimensions={0} | all-to-all | bytes 5242880 | tf_op jit(solution)/shard_map/all_to_all | solution.py:183
  663.0 3.5 all-to-all-start.7
  666.5 5.1 fusion.81
  672.9 1.1 fusion.19
  674.0 0.9 fusion.53
  675.7 5.9 fusion.25
  681.6 33.7 %all-to-all-done.7 = bf16[128,64,128]{2,1,0:T(8,128)(2,1)} async-done(((bf16[128,64,128]{2,1,0:T(8,128)(2,1)}), bf16[128,64,128]{2,1,0:T(8,128)(2,1)}, u32[]{:S(2)}, u32[]{:S(2)}) %all-to-all-start.7) | async-done | bytes 2097184 | tf_op jit(solution)/shard_map/all_to_all | solution.py:183
  715.3 2.1 convert_reduce_fusion.6
  717.4 2.2 fusion.43
  719.7 2.5 fusion.46
  722.1 3.1 fusion.52
  725.5 1.5 copy-done.12
  727.0 6.4 fusion.34
  (129 shorter events, 6.2 us)
Async XLA Ops:
  0.0 10.4 %copy-start.30 = (f32[2,2,128]{2,1,0:T(2,128)S(1)}, f32[2,2,128]{2,1,0:T(2,128)}, u32[]{:S(2)}) copy-start(f32[2,2,128]{2,1,0:T(2,128)} %param.8) | copy-start | bytes 6148
  0.0 10.4 %copy-start.29 = (f32[2,2,128]{2,1,0:T(2,128)S(1)}, f32[2,2,128]{2,1,0:T(2,128)}, u32[]{:S(2)}) copy-start(f32[2,2,128]{2,1,0:T(2,128)} %param.9) | copy-start | bytes 6148
  1.1 12.9 %copy-start.14 = (bf16[128,640]{1,0:T(8,128)(2,1)}, bf16[128,640]{1,0:T(8,128)(2,1)S(1)}, u32[]{:S(2)}) copy-start(bf16[128,640]{1,0:T(8,128)(2,1)S(1)} %get-tuple-element.22) | copy-start | bytes 491524
  1.9 9.2 %copy-start.6 = (bf16[96,192,128]{2,1,0:T(8,128)(2,1)S(1)}, bf16[96,192,128]{2,1,0:T(8,128)(2,1)}, u32[]{:S(2)}) copy-start(bf16[96,192,128]{2,1,0:T(8,128)(2,1)} %param.6) | copy-start | bytes 14155780
  10.3 3.7 copy-start.17
  10.4 21.1 %copy-start.13 = (f32[96,192,1]{1,0,2:T(8,128)}, f32[96,192,1]{1,0,2:T(8,128)S(1)}, u32[]{:S(2)}) copy-start(f32[96,192,1]{1,0,2:T(8,128)S(1)} %broadcast_multiply_fusion) | copy-start | bytes 221188
  11.0 2.9 copy-start.31
  11.0 2.9 copy-start.35
  22.4 9.1 %slice-start.4 = ((bf16[96,192,128]{2,1,0:T(8,128)(2,1)}), bf16[96,64,128]{2,1,0:T(8,128)(2,1)S(1)}, s32[]{:S(2)}) async-start(bf16[96,192,128]{2,1,0:T(8,128)(2,1)} %param.6), calls=%async_computation.12 | async-start | bytes 3145728 | tf_op jit(solution)/shard_map/slice | solution.py:198
  22.4 68.0 %all-to-all-start = ((bf16[128,80,128]{2,1,0:T(8,128)(2,1)}), bf16[128,80,128]{2,1,0:T(8,128)(2,1)}, u32[]{:S(2)}, u32[]{:S(2)}) async-start(bf16[128,80,128]{2,1,0:T(8,128)(2,1)} %copy.29), calls=%async_computation | async-start | bytes 5242880 | tf_op jit(solution)/shard_map/all_to_all | solution.py:183
  31.5 0.9 copy-start.7
  31.5 3.5 slice-start.5
  31.5 3.6 slice-start.6
  31.7 17.0 %copy-start.4 = (bf16[2,48,64,128]{3,2,0,1:T(8,128)(2,1)}, bf16[2,48,64,128]{3,2,0,1:T(8,128)(2,1)S(1)}, u32[]{:S(2)}) copy-start(bf16[2,48,64,128]{3,2,0,1:T(8,128)(2,1)S(1)} %copy.31) | copy-start | bytes 4718596
  34.9 4.5 copy-start.8
  34.9 4.5 copy-start.15
  35.0 4.5 copy-start.32
  35.0 4.5 copy-start.36
  35.1 13.6 %copy-start.19 = (f32[64,128]{1,0:T(8,128)}, f32[64,128]{1,0:T(8,128)S(1)}, u32[]{:S(2)}) copy-start(f32[64,128]{1,0:T(8,128)S(1)} %fusion.67) | copy-start | bytes 98308
  35.1 6.7 slice-start
  39.4 2.4 slice-start.1
  39.4 2.4 copy-start.18
  254.5 3.1 copy-start.33
  254.5 3.1 copy-start.37
  254.5 63.1 %all-to-all-start.2 = ((bf16[128,80,128]{2,1,0:T(8,128)(2,1)}), bf16[128,80,128]{2,1,0:T(8,128)(2,1)S(1)}, u32[]{:S(2)}, u32[]{:S(2)}) async-start(bf16[128,80,128]{2,1,0:T(8,128)(2,1)} %bitcast.21), calls=%async_computation.2 | async-start | bytes 5242880 | tf_op jit(solution)/shard_map/all_to_all | solution.py:183
  317.6 5.6 copy-start.27
  317.6 5.6 copy-start.28
  317.6 53.1 %all-to-all-start.4 = ((bf16[128,64,128]{2,1,0:T(8,128)(2,1)}), bf16[128,64,128]{2,1,0:T(8,128)(2,1)}, u32[]{:S(2)}, u32[]{:S(2)}) async-start(bf16[128,64,128]{2,1,0:T(8,128)(2,1)} %bitcast.22), calls=%async_computation.4 | async-start | bytes 4194304 | tf_op jit(solution)/shard_map/all_to_all | solution.py:183
  322.4 1.9 copy-start.16
  323.2 2.0 slice-start.2
  324.3 2.2 slice-start.3
  324.3 2.2 copy-start.34
  324.4 2.2 copy-start.38
  326.5 9.7 %copy-start.21 = (f32[128]{0:T(128)S(1)}, f32[128]{0:T(128)}, u32[]{:S(2)}) copy-start(f32[128]{0:T(128)} %get-tuple-element.30) | copy-start | bytes 1540
  326.5 9.7 %copy-start.23 = (f32[128]{0:T(128)S(1)}, f32[128]{0:T(128)}, u32[]{:S(2)}) copy-start(f32[128]{0:T(128)} %get-tuple-element.35) | copy-start | bytes 1540
  332.9 20.5 %copy-start.2 = (bf16[80,128,128]{2,1,0:T(8,128)(2,1)}, bf16[80,128,128]{2,1,0:T(8,128)(2,1)S(1)}, u32[]{:S(2)}) copy-start(bf16[80,128,128]{2,1,0:T(8,128)(2,1)S(1)} %get-tuple-element.34) | copy-start | bytes 7864324
  370.7 64.4 %all-to-all-start.3 = ((bf16[128,80,128]{2,1,0:T(8,128)(2,1)}), bf16[128,80,128]{2,1,0:T(8,128)(2,1)S(1)}, u32[]{:S(2)}, u32[]{:S(2)}) async-start(bf16[128,80,128]{2,1,0:T(8,128)(2,1)} %copy.34), calls=%async_computation.3 | async-start | bytes 5242880 | tf_op jit(solution)/shard_map/all_to_all | solution.py:183
  375.0 7.0 copy-start.5
  375.0 7.0 copy-start.39
  382.0 8.7 %copy-start.22 = (f32[128]{0:T(128)S(1)}, f32[128]{0:T(128)}, u32[]{:S(2)}) copy-start(f32[128]{0:T(128)} %get-tuple-element.30) | copy-start | bytes 1540
  382.0 8.7 %copy-start.24 = (f32[128]{0:T(128)S(1)}, f32[128]{0:T(128)}, u32[]{:S(2)}) copy-start(f32[128]{0:T(128)} %get-tuple-element.35) | copy-start | bytes 1540
  388.3 11.2 %copy-start = (bf16[64,128,128]{2,1,0:T(8,128)(2,1)}, bf16[64,128,128]{2,1,0:T(8,128)(2,1)S(1)}, u32[]{:S(2)}) copy-start(bf16[64,128,128]{2,1,0:T(8,128)(2,1)S(1)} %get-tuple-element.32) | copy-start | bytes 6291460
  393.1 2.4 copy-start.20
  399.5 4.0 copy-start.11
  435.1 155.0 %copy-start.10 = (bf16[128,80,128]{2,1,0:T(8,128)(2,1)}, bf16[128,80,128]{2,1,0:T(8,128)(2,1)S(1)}, u32[]{:S(2)}) copy-start(bf16[128,80,128]{2,1,0:T(8,128)(2,1)S(1)} %all-to-all-done.3) | copy-start | bytes 7864324
  663.0 52.3 %all-to-all-start.7 = ((bf16[128,64,128]{2,1,0:T(8,128)(2,1)}), bf16[128,64,128]{2,1,0:T(8,128)(2,1)}, u32[]{:S(2)}, u32[]{:S(2)}) async-start(bf16[128,64,128]{2,1,0:T(8,128)(2,1)} %bitcast.42), calls=%async_computation.7 | async-start | bytes 4194304 | tf_op jit(solution)/shard_map/all_to_all | solution.py:183
  671.7 1.2 copy-start.25
  671.7 1.2 copy-start.26
  674.0 1.7 copy-start.3
  681.6 40.5 %copy-start.1 = (bf16[64,128,128]{2,1,0:T(8,128)(2,1)S(1)}, bf16[64,128,128]{2,1,0:T(8,128)(2,1)}, u32[]{:S(2)}) copy-start(bf16[64,128,128]{2,1,0:T(8,128)(2,1)} %copy-done) | copy-start | bytes 6291460
  715.3 6.8 copy-start.9
  725.3 1.7 copy-start.12

commit v5 on v4

--- a/solution.py
+++ b/solution.py
@@ -212,10 +212,14 @@
         left_first = exchange(left[0])
         others = jnp.concatenate([left[1], right[0], right[1]], axis=1)
         products = triangle(left_first, exchange(others), geometry, update_index == 1)
-        returned_first = exchange(products[0])
-        returned_first, second = lax.optimization_barrier((returned_first, products[1]))
+        lead = update_index
+        leading = exchange(products[lead])
+        leading, other = lax.optimization_barrier((leading, products[1 - lead]))
+        arrived = [leading, exchange(other)]
+        if lead == 1:
+            arrived.reverse()
         later = []
-        for state, normed_part, returned in zip(states, normed, (returned_first, exchange(second))):
+        for state, normed_part, returned in zip(states, normed, arrived):
             normed_out = layer_norm(
                 returned, gain_out[:, None, None], bias_out[:, None, None], 0
             ).astype(jnp.bfloat16)

time: 739 us -> 736 us (level)
  waiting for transfers between devices: 136 us -> 150 us
  blocking collectives: 373 us -> 361 us
    all_to_all x5, waiting for transfers between devices: 136 us -> 150 us  [exchange(): lax.all_to_all(block, ('row', 'col'), split_axis=0, concat_axis=0, tiled=...]
    all_to_all x3, blocking collectives: 373 us -> 361 us  [exchange(): lax.all_to_all(block, ('row', 'col'), split_axis=0, concat_axis=0, tiled=...]
where the time goes in v5:
time: 736 us; the launch traced here: 731 us
  blocking collectives  361 us (49%)
  waiting for transfers between devices  150 us (20%)
  matrix products  94.5 us (13%)
  other arithmetic  44.9 us (6%)
  local copies, waits for them, and re-layouts  36.2 us (5%)
  starting transfers between devices  23.4 us (3%)
  Pallas kernels  19 us (3%)
    all_to_all x3, blocking collectives, exchange(): lax.all_to_all(block, ('row', 'col'), split_axis=0, concat_axis=0, tiled=...  361 us
    all_to_all x5, waiting for transfers between devices, exchange(): lax.all_to_all(block, ('row', 'col'), split_axis=0, concat_axis=0, tiled=...  150 us
    dot_general x16, matrix products, project(): jnp.einsum('ijc,cd->dij', normed, block, preferred_element_type=jnp.float32)  62.5 us
    all_to_all x5, starting transfers between devices, exchange(): lax.all_to_all(block, ('row', 'col'), split_axis=0, concat_axis=0, tiled=...  23.4 us
    dot_general x4, matrix products, packed_body(): jnp.einsum('ijc,cd->ijd', normed_part, weights_in[:, 4 * channels:5 * cha...  21 us
    concatenate x2, local copies, waits for them, and re-layouts, packed_body(): others = jnp.concatenate([left[1], right[0], right[1]], axis=1)  20.4 us
    pallas_call x2, Pallas kernels, triangle(): pl.pallas_call(functools.partial(triangle_kernel, geometry, incoming), gr...  19 us
    reduce_sum x8, other arithmetic, layer_norm(): variance = jnp.mean(centred * centred, axis=axis_pos, keepdims=True)  17.4 us
  transfers between devices with their start and end apart: 5, of which 5 were waited for; matrix products, arithmetic and copies ran while one was open for 19% of the time, Pallas kernels for 0%

profile of v5, /device:TPU:0, one launch (start us, length us, event | category | flops | bytes accessed | tf_op | source)
XLA Modules:
  0.0 730.6 jit_solution(11112841934912389919)
XLA Ops:
  0.0 1.1 slice_bitcast_fusion
  1.9 0.9 select_reduce_fusion.1
  2.8 2.7 convert_reduce_fusion.1
  5.6 4.7 fusion.12
  11.0 2.9 fusion.78
  14.0 5.2 fusion.57
  19.2 3.2 copy.29
  22.4 8.0 %all-to-all-start = ((bf16[128,80,128]{2,1,0:T(8,128)(2,1)}), bf16[128,80,128]{2,1,0:T(8,128)(2,1)}, u32[]{:S(2)}, u32[]{:S(2)}) async-start(bf16[128,80,128]{2,1,0:T(8,128)(2,1)} %copy.29), calls=%async_computation | async-start | bytes 5242880 | tf_op jit(solution)/shard_map/all_to_all | solution.py:183
  30.4 1.1 slice.120
  32.3 2.6 fusion.39
  35.1 4.2 fusion.77
  39.4 2.4 fusion.79
  41.8 2.9 fusion.80
  44.7 4.0 fusion.63
  48.7 4.0 fusion.64
  52.7 5.1 fusion.58
  57.9 3.5 pad_maximum_fusion
  61.4 10.1 %copy.32 = bf16[128,208,128]{2,1,0:T(8,128)(2,1)} copy(bf16[128,208,128]{0,2,1:T(8,128)(2,1)} %pad_maximum_fusion) | data formatting | bytes 13631488 | tf_op jit(solution)/shard_map/concatenate | solution.py:213
  71.5 18.9 %all-to-all-done = bf16[128,80,128]{2,1,0:T(8,128)(2,1)} async-done(((bf16[128,80,128]{2,1,0:T(8,128)(2,1)}), bf16[128,80,128]{2,1,0:T(8,128)(2,1)}, u32[]{:S(2)}, u32[]{:S(2)}) %all-to-all-start) | async-done | bytes 2621472 | tf_op jit(solution)/shard_map/all_to_all | solution.py:183
  90.4 154.6 %all_to_all.40 = bf16[128,208,128]{2,1,0:T(8,128)(2,1)} all-to-all(bf16[128,208,128]{2,1,0:T(8,128)(2,1)} %copy.32), channel_id=1, replica_groups=mesh['row'=8,'col'=4] {'row','col'}, dimensions={0} | all-to-all | bytes 13631488 | tf_op jit(solution)/shard_map/all_to_all | solution.py:183
  245.0 9.4 %triangle_out.1 = (bf16[8,4,4,80,128]{4,3,2,1,0:T(8,128)(2,1)}, bf16[8,4,4,64,128]{4,3,2,1,0:T(8,128)(2,1)}) custom-call(bf16[8,4,4,80,128]{4,3,2,1,0:T(8,128)(2,1)} %bitcast.8.refs_0_, bf16[8,4,4,208,128]{4,3,2,1,0:T(8,128)(2,1)} %bitcast.132), custom_call_target="tpu_custom_call" | custom-call | flops 3623878656 | bytes 14155776 | tf_op jit(solution)/shard_map/triangle_out/pallas_call | solution.py:136
  254.5 3.1 all-to-all-start.2
  257.6 5.1 fusion.76
  262.6 55.0 %all-to-all-done.2 = bf16[128,80,128]{2,1,0:T(8,128)(2,1)S(1)} async-done(((bf16[128,80,128]{2,1,0:T(8,128)(2,1)}), bf16[128,80,128]{2,1,0:T(8,128)(2,1)S(1)}, u32[]{:S(2)}, u32[]{:S(2)}) %all-to-all-start.2) | async-done | bytes 2621472 | tf_op jit(solution)/shard_map/all_to_all | solution.py:183
  317.6 4.4 all-to-all-start.4
  323.2 1.1 fusion.23
  324.3 0.9 fusion.55
  325.2 1.3 slice-done.3
  326.5 6.4 convert_reduce_fusion
  332.9 3.3 fusion.8
  336.2 2.9 fusion.83
  339.1 6.6 fusion.59
  345.8 4.7 copy.34
  350.5 2.9 fusion.85
  353.4 6.7 fusion.60
  360.0 10.6 %all-to-all-done.4 = bf16[128,64,128]{2,1,0:T(8,128)(2,1)} async-done(((bf16[128,64,128]{2,1,0:T(8,128)(2,1)}), bf16[128,64,128]{2,1,0:T(8,128)(2,1)}, u32[]{:S(2)}, u32[]{:S(2)}) %all-to-all-start.4) | async-done | bytes 2097184 | tf_op jit(solution)/shard_map/all_to_all | solution.py:183
  370.7 4.3 all-to-all-start.3
  375.0 2.1 convert_reduce_fusion.7
  377.1 2.4 fusion.47
  379.5 2.5 fusion.50
  382.0 6.3 convert_reduce_fusion.4
  388.3 2.4 fusion.35
  390.7 2.4 fusion.82
  393.1 2.4 fusion.84
  395.5 4.0 fusion.65
  399.5 4.0 fusion.66
  403.5 3.5 pad_maximum_fusion.1
  407.0 10.2 %copy.36 = bf16[128,208,128]{2,1,0:T(8,128)(2,1)} copy(bf16[128,208,128]{0,2,1:T(8,128)(2,1)} %pad_maximum_fusion.1) | data formatting | bytes 13631488 | tf_op jit(solution)/shard_map/concatenate | solution.py:213
  417.2 17.8 %all-to-all-done.3 = bf16[128,80,128]{2,1,0:T(8,128)(2,1)S(1)} async-done(((bf16[128,80,128]{2,1,0:T(8,128)(2,1)}), bf16[128,80,128]{2,1,0:T(8,128)(2,1)S(1)}, u32[]{:S(2)}, u32[]{:S(2)}) %all-to-all-start.3) | async-done | bytes 2621472 | tf_op jit(solution)/shard_map/all_to_all | solution.py:183
  435.0 155.0 %all_to_all.41 = bf16[128,208,128]{2,1,0:T(8,128)(2,1)} all-to-all(bf16[128,208,128]{2,1,0:T(8,128)(2,1)} %copy.36), channel_id=1, replica_groups=mesh['row'=8,'col'=4] {'row','col'}, dimensions={0} | all-to-all | bytes 13631488 | tf_op jit(solution)/shard_map/all_to_all | solution.py:183
  590.1 9.5 %triangle_in.1 = (bf16[8,4,4,80,128]{4,3,2,1,0:T(8,128)(2,1)}, bf16[8,4,4,64,128]{4,3,2,1,0:T(8,128)(2,1)S(1)}) custom-call(bf16[8,4,4,80,128]{4,3,2,1,0:T(8,128)(2,1)} %bitcast.136, bf16[8,4,4,208,128]{4,3,2,1,0:T(8,128)(2,1)} %bitcast.133), custom_call_target="tpu_custom_call" | custom-call | flops 3623878656 | bytes 14155776 | tf_op jit(solution)/shard_map/triangle_in/pallas_call | solution.py:136
  599.6 51.6 %all_to_all.42 = bf16[128,64,128]{2,1,0:T(8,128)(2,1)} all-to-all(bf16[128,64,128]{2,1,0:T(8,128)(2,1)S(1)} %bitcast.118), channel_id=1, replica_groups=mesh['row'=8,'col'=4] {'row','col'}, dimensions={0} | all-to-all | bytes 4194304 | tf_op jit(solution)/shard_map/all_to_all | solution.py:183
  651.3 3.7 all-to-all-start.7
  655.0 4.5 fusion.81
  660.5 0.9 fusion.46
  661.4 3.1 fusion.52
  664.6 1.1 copy-done.8
  665.8 1.3 copy.39
  667.1 47.9 %all-to-all-done.7 = bf16[128,80,128]{2,1,0:T(8,128)(2,1)S(1)} async-done(((bf16[128,80,128]{2,1,0:T(8,128)(2,1)}), bf16[128,80,128]{2,1,0:T(8,128)(2,1)S(1)}, u32[]{:S(2)}, u32[]{:S(2)}) %all-to-all-start.7) | async-done | bytes 2621472 | tf_op jit(solution)/shard_map/all_to_all | solution.py:183
  716.2 1.1 fusion.19
  717.3 0.9 fusion.53
  718.1 0.8 copy-done.4
  719.0 5.0 fusion.25
  724.1 6.4 fusion.34
  (133 shorter events, 6.2 us)
Async XLA Ops:
  0.0 10.4 %copy-start.32 = (f32[2,2,128]{2,1,0:T(2,128)S(1)}, f32[2,2,128]{2,1,0:T(2,128)}, u32[]{:S(2)}) copy-start(f32[2,2,128]{2,1,0:T(2,128)} %param.8) | copy-start | bytes 6148
  0.0 10.4 %copy-start.31 = (f32[2,2,128]{2,1,0:T(2,128)S(1)}, f32[2,2,128]{2,1,0:T(2,128)}, u32[]{:S(2)}) copy-start(f32[2,2,128]{2,1,0:T(2,128)} %param.9) | copy-start | bytes 6148
  1.1 12.9 %copy-start.16 = (bf16[128,640]{1,0:T(8,128)(2,1)}, bf16[128,640]{1,0:T(8,128)(2,1)S(1)}, u32[]{:S(2)}) copy-start(bf16[128,640]{1,0:T(8,128)(2,1)S(1)} %get-tuple-element.22) | copy-start | bytes 491524
  1.9 9.2 %copy-start.7 = (bf16[96,192,128]{2,1,0:T(8,128)(2,1)S(1)}, bf16[96,192,128]{2,1,0:T(8,128)(2,1)}, u32[]{:S(2)}) copy-start(bf16[96,192,128]{2,1,0:T(8,128)(2,1)} %param.6) | copy-start | bytes 14155780
  10.3 3.7 copy-start.19
  10.4 21.1 %copy-start.15 = (f32[96,192,1]{1,0,2:T(8,128)}, f32[96,192,1]{1,0,2:T(8,128)S(1)}, u32[]{:S(2)}) copy-start(f32[96,192,1]{1,0,2:T(8,128)S(1)} %broadcast_multiply_fusion) | copy-start | bytes 221188
  11.0 2.9 copy-start.33
  11.0 2.9 copy-start.37
  22.4 9.1 %slice-start.4 = ((bf16[96,192,128]{2,1,0:T(8,128)(2,1)}), bf16[96,64,128]{2,1,0:T(8,128)(2,1)S(1)}, s32[]{:S(2)}) async-start(bf16[96,192,128]{2,1,0:T(8,128)(2,1)} %param.6), calls=%async_computation.12 | async-start | bytes 3145728 | tf_op jit(solution)/shard_map/slice | solution.py:198
  22.4 68.0 %all-to-all-start = ((bf16[128,80,128]{2,1,0:T(8,128)(2,1)}), bf16[128,80,128]{2,1,0:T(8,128)(2,1)}, u32[]{:S(2)}, u32[]{:S(2)}) async-start(bf16[128,80,128]{2,1,0:T(8,128)(2,1)} %copy.29), calls=%async_computation | async-start | bytes 5242880 | tf_op jit(solution)/shard_map/all_to_all | solution.py:183
  31.5 0.9 copy-start.11
  31.5 3.5 slice-start.5
  31.5 3.6 slice-start.6
  31.7 17.0 %copy-start.5 = (bf16[2,48,64,128]{3,2,0,1:T(8,128)(2,1)}, bf16[2,48,64,128]{3,2,0,1:T(8,128)(2,1)S(1)}, u32[]{:S(2)}) copy-start(bf16[2,48,64,128]{3,2,0,1:T(8,128)(2,1)S(1)} %copy.31) | copy-start | bytes 4718596
  34.9 4.5 copy-start.12
  34.9 4.5 copy-start.17
  34.9 4.5 copy-start.34
  35.0 4.5 copy-start.38
  35.1 13.6 %copy-start.21 = (f32[64,128]{1,0:T(8,128)}, f32[64,128]{1,0:T(8,128)S(1)}, u32[]{:S(2)}) copy-start(f32[64,128]{1,0:T(8,128)S(1)} %fusion.67) | copy-start | bytes 98308
  35.1 6.7 slice-start
  39.4 2.4 slice-start.1
  39.4 2.4 copy-start.20
  254.5 3.1 copy-start.35
  254.5 3.1 copy-start.39
  254.5 63.1 %all-to-all-start.2 = ((bf16[128,80,128]{2,1,0:T(8,128)(2,1)}), bf16[128,80,128]{2,1,0:T(8,128)(2,1)S(1)}, u32[]{:S(2)}, u32[]{:S(2)}) async-start(bf16[128,80,128]{2,1,0:T(8,128)(2,1)} %bitcast.21), calls=%async_computation.2 | async-start | bytes 5242880 | tf_op jit(solution)/shard_map/all_to_all | solution.py:183
  317.6 5.6 copy-start.29
  317.6 5.6 copy-start.30
  317.6 53.1 %all-to-all-start.4 = ((bf16[128,64,128]{2,1,0:T(8,128)(2,1)}), bf16[128,64,128]{2,1,0:T(8,128)(2,1)}, u32[]{:S(2)}, u32[]{:S(2)}) async-start(bf16[128,64,128]{2,1,0:T(8,128)(2,1)} %bitcast.22), calls=%async_computation.4 | async-start | bytes 4194304 | tf_op jit(solution)/shard_map/all_to_all | solution.py:183
  322.4 1.9 copy-start.18
  323.2 2.0 slice-start.2
  324.3 2.2 slice-start.3
  324.3 2.2 copy-start.36
  324.3 2.2 copy-start.40
  326.5 9.7 %copy-start.23 = (f32[128]{0:T(128)S(1)}, f32[128]{0:T(128)}, u32[]{:S(2)}) copy-start(f32[128]{0:T(128)} %get-tuple-element.30) | copy-start | bytes 1540
  326.5 9.7 %copy-start.25 = (f32[128]{0:T(128)S(1)}, f32[128]{0:T(128)}, u32[]{:S(2)}) copy-start(f32[128]{0:T(128)} %get-tuple-element.35) | copy-start | bytes 1540
  332.9 20.5 %copy-start.3 = (bf16[80,128,128]{2,1,0:T(8,128)(2,1)}, bf16[80,128,128]{2,1,0:T(8,128)(2,1)S(1)}, u32[]{:S(2)}) copy-start(bf16[80,128,128]{2,1,0:T(8,128)(2,1)S(1)} %get-tuple-element.34) | copy-start | bytes 7864324
  370.7 64.4 %all-to-all-start.3 = ((bf16[128,80,128]{2,1,0:T(8,128)(2,1)}), bf16[128,80,128]{2,1,0:T(8,128)(2,1)S(1)}, u32[]{:S(2)}, u32[]{:S(2)}) async-start(bf16[128,80,128]{2,1,0:T(8,128)(2,1)} %copy.34), calls=%async_computation.3 | async-start | bytes 5242880 | tf_op jit(solution)/shard_map/all_to_all | solution.py:183
  375.0 7.0 copy-start.6
  375.0 7.0 copy-start.41
  382.0 8.7 %copy-start.24 = (f32[128]{0:T(128)S(1)}, f32[128]{0:T(128)}, u32[]{:S(2)}) copy-start(f32[128]{0:T(128)} %get-tuple-element.30) | copy-start | bytes 1540
  382.0 8.7 %copy-start.26 = (f32[128]{0:T(128)S(1)}, f32[128]{0:T(128)}, u32[]{:S(2)}) copy-start(f32[128]{0:T(128)} %get-tuple-element.35) | copy-start | bytes 1540
  388.3 11.2 %copy-start.1 = (bf16[64,128,128]{2,1,0:T(8,128)(2,1)}, bf16[64,128,128]{2,1,0:T(8,128)(2,1)S(1)}, u32[]{:S(2)}) copy-start(bf16[64,128,128]{2,1,0:T(8,128)(2,1)S(1)} %get-tuple-element.32) | copy-start | bytes 6291460
  393.1 2.4 copy-start.22
  399.5 4.0 copy-start.14
  435.0 155.0 %copy-start.13 = (bf16[128,80,128]{2,1,0:T(8,128)(2,1)}, bf16[128,80,128]{2,1,0:T(8,128)(2,1)S(1)}, u32[]{:S(2)}) copy-start(bf16[128,80,128]{2,1,0:T(8,128)(2,1)S(1)} %all-to-all-done.3) | copy-start | bytes 7864324
  651.3 63.7 %all-to-all-start.7 = ((bf16[128,80,128]{2,1,0:T(8,128)(2,1)}), bf16[128,80,128]{2,1,0:T(8,128)(2,1)S(1)}, u32[]{:S(2)}, u32[]{:S(2)}) async-start(bf16[128,80,128]{2,1,0:T(8,128)(2,1)} %bitcast.42), calls=%async_computation.7 | async-start | bytes 5242880 | tf_op jit(solution)/shard_map/all_to_all | solution.py:183
  654.9 4.5 copy-start
  654.9 5.5 copy-start.27
  654.9 5.5 copy-start.28
  659.5 1.9 copy-start.2
  664.4 1.3 copy-start.8
  717.3 1.7 copy-start.4
  719.0 5.0 copy-start.9
  719.0 5.1 copy-start.10
